TPU v7x, 32 devices: a whole 2x2x4 slice. The times are simulated.
32 devices in a mesh: wheel: 16 (over z, x, core), slab: 2 (over y).
Axes of the slice: x: 2, y: 2, z: 4, core: 2. Of those that a mesh axis runs over, the one named last changes fastest.
Arguments:
- krylov_block: float32 [2, 32, 3, 16, 512], P(None, 'wheel', None, None, 'slab'), may hold values from -6 to 6
- blade_class: int32 [32], P('wheel'), may hold values from 0 to 3
- neighbors: int32 [8, 512], P(None, 'slab'), may hold values from 0 to 511
- iface_rows: int32 [2, 128], P(None, 'slab'), may hold values from 0 to 255
- face_rows: int32 [2, 128], P(None, 'slab'), may hold values from 0 to 255
- stiffness: float32 [3, 3, 8, 512], P(None, None, None, 'slab'), may hold values from -1.25 to 1.25
- lumped_mass: float32 [3, 512], P(None, 'slab'), may hold values from 0.5 to 2
- precond: bfloat16 [16, 16, 384, 384], P('wheel', 'slab'), may hold values from -0.3125 to 0.3125
Outputs:
- preconditioned: float32 [16, 16, 16, 384], P('wheel', 'slab')
Inputs may be any that keep to these rules, and one draw needn't show every extreme that they name: `neighbors`: extended numbering: own nodes first (256), then 64 from the lower slab, 64 from the upper slab, 64 from the previous sector, 64 from the next sector.
All inputs are finite; a program needn't handle non-finite values.
Results may differ from a plain program's by a relative error of at most 0.0039.
Values may be sent and summed in bfloat16 or wider, within the bound.
No kernel may reach another device: no remote copies, remote signals or barrier semaphores. Data moves between devices by JAX's collectives and lax.ppermute only.
A program may use at most 64 MiB of HBM per device.

v0:
```python
import math

import jax
import jax.numpy as jnp
from jax import lax
from jax.sharding import PartitionSpec as P

GROUP = 32


damping_ratio = 0.5
gyro_rate = 0.8
shift_value = 0.3
class_step = 0.125


def extended_2(block, sides, width, periodic):
    for axis, dim in sides:
        count = lax.axis_size(axis)
        forward = [(i, i + 1) for i in range(count - 1)]
        if periodic:
            forward.append((count - 1, 0))
        backward = [(target, source) for source, target in forward]
        low = lax.ppermute(
            lax.slice_in_dim(block, block.shape[dim] - width, None, axis=dim), axis, forward
        )
        high = lax.ppermute(lax.slice_in_dim(block, 0, width, axis=dim), axis, backward)
        block = jnp.concatenate([low, block, high], axis=dim)
    return block


def basis(row_ids, col_ids, sectors_all):
    pair_id = row_ids[:, None] // 2
    part_id = row_ids[:, None] % 2
    sector_id = col_ids[None, :]
    phases = pair_id * sector_id % sectors_all
    angles = 2.0 * math.pi / sectors_all * phases.astype(jnp.float32)
    parity = (1 - 2 * (sector_id % 2)).astype(jnp.float32)
    edge_rows = jnp.where(
        part_id == 0, jnp.ones_like(angles), parity * jnp.ones_like(angles)
    ) * math.sqrt(1.0 / sectors_all)
    inner_rows = jnp.where(part_id == 0, jnp.cos(angles), jnp.sin(angles)) * math.sqrt(
        2.0 / sectors_all
    )
    return jnp.where(pair_id == 0, edge_rows, inner_rows)


def arrange(harmonic):
    pair_rows, states, comps, vectors, nodes = harmonic.shape
    shaped = harmonic.reshape(pair_rows // 2, 2, states, comps, vectors, nodes // GROUP, GROUP)
    shaped = shaped.transpose(0, 5, 4, 1, 2, 3, 6)
    return shaped.reshape(pair_rows // 2, nodes // GROUP, vectors, 4 * comps * GROUP)


def on_device(
    krylov_block, blade_class, neighbors, iface_rows, face_rows, stiffness, lumped_mass, precond
):
    displacement = krylov_block[0]
    velocity = krylov_block[1]
    moved_field = displacement + damping_ratio * velocity
    rim_width = iface_rows.shape[1]
    face_width = face_rows.shape[1]
    rims = jnp.concatenate(
        (
            jnp.take(moved_field, iface_rows[0], axis=3),
            jnp.take(moved_field, iface_rows[1], axis=3),
        ),
        axis=3,
    )
    rimmed = extended_2(rims.astype(jnp.bfloat16), (("slab", 3),), rim_width, False).astype(
        rims.dtype
    )
    from_lower = rimmed[..., :rim_width]
    from_upper = rimmed[..., 3 * rim_width :]
    left_face = jnp.take(moved_field, face_rows[0], axis=3)
    right_face = jnp.take(moved_field, face_rows[1], axis=3)
    edges = jnp.concatenate((left_face[0], right_face[-1]), axis=2)
    faced = extended_2(edges, (("wheel", 2),), face_width, True)
    from_prev = jnp.concatenate((faced[None, :, :, :face_width], right_face[:-1]), axis=0)
    from_next = jnp.concatenate((left_face[1:], faced[None, :, :, 3 * face_width :]), axis=0)
    extended = jnp.concatenate((moved_field, from_lower, from_upper, from_prev, from_next), axis=3)
    picked = jnp.take(extended, neighbors, axis=3)
    restore = jnp.einsum("cdkn,sdvkn->scvn", stiffness, picked, precision=lax.Precision.HIGHEST)
    scale = (1.0 + class_step * blade_class.astype(jnp.float32))[:, None, None, None]
    gyro = gyro_rate * jnp.stack(
        (
            -lumped_mass[0] * velocity[:, 1],
            lumped_mass[1] * velocity[:, 0],
            jnp.zeros_like(velocity[:, 2]),
        ),
        axis=1,
    )
    res_disp = velocity - shift_value * displacement
    res_velo = -scale * restore - gyro - shift_value * lumped_mass[None, :, None, :] * velocity
    residual = jnp.stack((res_disp, res_velo), axis=0)
    local_sectors = residual.shape[1]
    sectors_all = lax.axis_size("wheel") * local_sectors
    spread = lax.all_to_all(residual, "wheel", split_axis=4, concat_axis=1, tiled=True)
    table = basis(
        jnp.arange(sectors_all, dtype=jnp.int32),
        jnp.arange(sectors_all, dtype=jnp.int32),
        sectors_all,
    )
    transformed = jnp.einsum(
        "bs,tscvn->btcvn", table, spread, precision=lax.Precision.HIGHEST
    ).astype(jnp.bfloat16)
    harmonic = lax.all_to_all(transformed, "wheel", split_axis=0, concat_axis=4, tiled=True)
    lhs = arrange(harmonic)
    return jnp.einsum("pgvj,pgij->pgvi", lhs, precond, preferred_element_type=jnp.float32)


def solution(mesh):
    return jax.shard_map(
        on_device,
        mesh=mesh,
        in_specs=(
            P(None, "wheel", None, None, "slab"),
            P("wheel"),
            P(None, "slab"),
            P(None, "slab"),
            P(None, "slab"),
            P(None, None, None, "slab"),
            P(None, "slab"),
            P("wheel", "slab", None, None),
        ),
        out_specs=P("wheel", "slab", None, None),
        check_vma=False,
    )
```

profile of v0, /device:TPU:0, one launch (start us, length us, event | category | flops | bytes accessed | tf_op | source)
XLA Modules:
  0.0 120.3 jit_solution(17209610336945923455)
XLA Ops:
  0.0 1.1 bitcast_add_fusion
  1.1 0.5 copy.155
  1.6 1.4 %compare_and_fusion.4 = (pred[64]{0:T(512)(128)(4,1)}, s32[64]{0:T(128)S(1)}, pred[64]{0:T(512)(128)(4,1)}, s32[64]{0:T(128)}) fusion(s32[2,64]{1,0:T(2,128)} %param.13), kind=kLoop, calls=%fused_computation.77 | loop fusion | flops 768 | bytes 1152 | tf_op jit(solution)/shard_map/jit(_take)/and | solution.py:66
  3.0 0.8 gather_fusion.1
  3.8 0.7 copy.156
  4.5 1.4 %bitcast_convert_fusion.1 = bf16[2,3,16,64]{3,2,1,0:T(8,128)(2,1)} fusion(bf16[64,2,3,16]{0,3,2,1:T(8,128)(2,1)} %copy.156, pred[64]{0:T(512)(128)(4,1)} %get-tuple-element.10), kind=kLoop, calls=%fused_computation.26 | loop fusion | flops 6144 | bytes 24640 | tf_op jit(solution)/shard_map/slice | solution.py:25
  5.9 5.5 %collective-permute-start = (bf16[2,3,16,64]{3,2,1,0:T(8,128)(2,1)}, bf16[2,3,16,64]{3,2,1,0:T(8,128)(2,1)}, u32[]{:S(2)}, u32[]{:S(2)}) collective-permute-start(bf16[2,3,16,64]{3,2,1,0:T(8,128)(2,1)} %bitcast_convert_fusion.1), channel_id=1, source_target_pairs={{0,1},{2,3},{4,5},{6,7},{8,9},{10,11},{12,13},{14,15},{16,17},{18,... | collective-permute-start | bytes 36872 | tf_op jit(solution)/shard_map/ppermute | solution.py:24
  11.3 0.7 pad_clamp_fusion.2
  12.0 0.8 gather_fusion.2
  12.9 0.7 copy.158
  13.6 1.3 %bitcast_convert_fusion = bf16[2,3,16,64]{3,2,1,0:T(8,128)(2,1)} fusion(bf16[64,2,3,16]{0,3,2,1:T(8,128)(2,1)} %copy.158, pred[64]{0:T(512)(128)(4,1)} %get-tuple-element.28), kind=kLoop, calls=%fused_computation.25 | loop fusion | flops 6144 | bytes 24640 | tf_op jit(solution)/shard_map/slice | solution.py:27
  14.9 1.3 %collective-permute-start.1 = (bf16[2,3,16,64]{3,2,1,0:T(8,128)(2,1)}, bf16[2,3,16,64]{3,2,1,0:T(8,128)(2,1)}, u32[]{:S(2)}, u32[]{:S(2)}) collective-permute-start(bf16[2,3,16,64]{3,2,1,0:T(8,128)(2,1)} %bitcast_convert_fusion), channel_id=1, source_target_pairs={{1,0},{3,2},{5,4},{7,6},{9,8},{11,10},{13,12},{15,14},{17,16},{19,... | collective-permute-start | bytes 36872 | tf_op jit(solution)/shard_map/ppermute | solution.py:27
  16.2 0.8 compare_and_fusion.1
  17.0 1.5 %gather_fusion.3 = f32[64,2,3,16]{3,1,2,0:T(2,128)} fusion(f32[2,3,16,256]{2,0,3,1:T(2,128)S(1)} %copy.155, s32[1024]{0:T(1024)S(1)} %pad_clamp_fusion.1), kind=kCustom, calls=%fused_computation.2.clone | custom fusion | bytes 49408 | tf_op jit(solution)/shard_map/jit(_take)/gather | solution.py:76
  18.5 1.0 copy.160
  19.5 1.5 %gather_fusion.4 = f32[64,2,3,16]{3,1,2,0:T(2,128)} fusion(f32[2,3,16,256]{2,0,3,1:T(2,128)S(1)} %copy.155, s32[1024]{0:T(1024)S(1)} %pad_clamp_fusion), kind=kCustom, calls=%fused_computation.3.clone | custom fusion | bytes 49408 | tf_op jit(solution)/shard_map/jit(_take)/gather | solution.py:75
  21.0 1.0 copy.162
  22.0 3.7 %collective-permute-start.3 = (f32[3,16,64]{2,1,0:T(8,128)S(1)}, f32[3,16,64]{2,1,0:T(8,128)S(1)}, u32[]{:S(2)}, u32[]{:S(2)}) collective-permute-start(f32[3,16,64]{2,1,0:T(8,128)S(1)} %get-tuple-element.21), channel_id=1, source_target_pairs={{2,0},{4,2},{6,4},{8,6},{10,8},{12,10},{14,12},{16,14},{18,16},{20... | collective-permute-start | bytes 36872 | tf_op jit(solution)/shard_map/ppermute | solution.py:27
  25.8 0.7 multiply_subtract_fusion
  26.5 0.6 slice_multiply_fusion.1
  27.2 0.7 add_negate_fusion
  27.8 2.2 %copy.173 = f32[3,3,8,256,1]{2,0,1,4,3:T(4,128)} copy(f32[3,3,8,256,1]{3,2,1,0,4:T(8,128)} %bitcast.88) | data formatting | bytes 147456 | tf_op args[5]
  30.3 0.9 maximum_convert_fusion
  31.3 0.5 collective-permute-done.2
  31.9 2.1 %copy.163 = f32[2,3,16,512]{2,0,3,1:T(2,128)} copy(f32[2,3,16,512]{3,2,1,0:T(8,128)S(1)} %concatenate.18) | data formatting | bytes 393216 | tf_op jit(solution)/shard_map/concatenate | solution.py:81
  33.9 23.2 %gather_fusion = f32[2048,2,3,16]{3,1,2,0:T(2,128)} fusion(f32[2,3,16,512]{2,0,3,1:T(2,128)} %copy.163, s32[2048]{0:T(1024)S(1)} %broadcast_clamp_fusion), kind=kCustom, calls=%fused_computation.4 | custom fusion | bytes 1581056 | tf_op jit(solution)/shard_map/jit(_take)/gather | solution.py:82
  57.1 10.7 %fusion.6 = f32[256,2,16,3]{2,3,1,0:T(4,128)S(1)} fusion(f32[3,3,8,256,1]{2,0,1,4,3:T(4,128)} %copy.173, f32[8,256,2,3,16]{4,2,3,1,0:T(2,128)} %bitcast.80, pred[8,256]{0,1:T(8,128)(4,1)S(1)} %copy.154), kind=kOutput, calls=%fused_computation.12 | convolution fusion | flops 7274496 | bytes 960512 | tf_op jit(solution)/shard_map/cdkn,sdvkn->scvn/dot_general | solution.py:83
  67.9 0.4 copy.166
  68.3 1.0 fusion.14
  69.3 0.9 pad_maximum_fusion
  70.2 2.2 %copy.167 = f32[2,2,3,16,256]{3,1,2,0,4:T(2,128)} copy(f32[2,2,3,16,256]{4,3,2,1,0:T(8,128)S(1)} %pad_maximum_fusion) | data formatting | bytes 393216 | tf_op jit(solution)/shard_map/stack | solution.py:95
  72.3 4.2 %reshape.174 = f32[16,1,3072]{2,1,0:T(1,128)} reshape(f32[256,2,3,2,16]{4,3,2,1,0:T(2,128)} %bitcast.81) | data formatting | bytes 393216
  76.6 5.4 %all-to-all-start = ((f32[16,1,3072]{2,1,0:T(1,128)}), f32[16,1,3072]{2,1,0:T(1,128)S(1)}, u32[]{:S(2)}, u32[]{:S(2)}) async-start(f32[16,1,3072]{2,1,0:T(1,128)} %reshape.174), calls=%async_computation | async-start | bytes 393216 | tf_op jit(solution)/shard_map/all_to_all | solution.py:98
  82.0 8.9 %all-to-all-done = f32[16,1,3072]{2,1,0:T(1,128)S(1)} async-done(((f32[16,1,3072]{2,1,0:T(1,128)}), f32[16,1,3072]{2,1,0:T(1,128)S(1)}, u32[]{:S(2)}, u32[]{:S(2)}) %all-to-all-start) | async-done | bytes 196640 | tf_op jit(solution)/shard_map/all_to_all | solution.py:98
  90.9 0.5 broadcast.231
  91.4 1.1 reduce
  92.5 3.3 %reshape.175 = f32[256,2,3,2,16]{4,3,2,1,0:T(2,128)} reshape(f32[16,3072]{1,0:T(8,128)S(1)} %reduce) | data formatting | bytes 393216
  95.8 3.7 %copy.168 = f32[2,2,3,16,16,16]{5,3,2,1,4,0:T(8,128)} copy(f32[2,2,3,16,16,16]{3,1,2,0,5,4:T(2,128)} %bitcast.82) | data formatting | bytes 393216 | tf_op jit(solution)/shard_map/all_to_all | solution.py:98
  99.5 2.0 %copy.169 = f32[2,32,3,16,16]{1,4,3,2,0:T(8,128)S(1)} copy(f32[2,32,3,16,16]{4,3,2,1,0:T(8,128)} %bitcast.83) | data formatting | bytes 393216 | tf_op jit(solution)/shard_map/all_to_all | solution.py:98
  101.4 0.9 fusion.18
  102.4 1.3 %copy.170 = bf16[32,2,3,16,16]{4,3,2,1,0:T(8,128)(2,1)S(1)} copy(bf16[32,2,3,16,16]{0,4,3,2,1:T(8,128)(2,1)S(1)} %convert_element_type.25) | data formatting | bytes 196608 | tf_op jit(solution)/shard_map/convert_element_type | solution.py:106
  103.7 0.8 reshape.176
  104.5 10.0 %all_to_all.33 = bf16[16,2,1536]{2,1,0:T(2,128)(2,1)S(1)} all-to-all(bf16[16,2,1536]{2,1,0:T(2,128)(2,1)S(1)} %reshape.176), channel_id=1, replica_groups=mesh['wheel'=16,'slab'=2] {'wheel'}, dimensions={0} | all-to-all | bytes 196608 | tf_op jit(solution)/shard_map/all_to_all | solution.py:107
  114.5 0.5 reshape.177
  115.0 1.4 %copy.171 = bf16[2,2,3,16,16,16]{5,4,3,2,1,0:T(8,128)(2,1)} copy(bf16[2,2,3,16,16,16]{5,3,2,1,0,4:T(8,128)(2,1)S(1)} %bitcast.85) | data formatting | bytes 196608 | tf_op jit(solution)/shard_map/all_to_all | solution.py:107
  116.4 1.7 %reshape.112 = bf16[1,2,2,3,16,8,32]{6,5,4,3,2,1,0:T(8,128)(2,1)S(1)} reshape(bf16[2,2,3,16,16,16]{5,4,3,2,1,0:T(8,128)(2,1)} %copy.171) | data formatting | bytes 196608 | tf_op jit(solution)/shard_map/reshape | solution.py:50
  118.1 0.3 copy.172
  118.8 1.5 %fusion.9 = f32[1,8,16,384]{3,2,1,0:T(8,128)} fusion(bf16[8,16,384]{2,1,0:T(8,128)(2,1)S(1)} %reshape.113, bf16[1,8,384,384]{3,2,1,0:T(8,128)(2,1)S(1)} %copy-done), kind=kOutput, calls=%fused_computation.13 | convolution fusion | flops 37748736 | bytes 2654208 | tf_op jit(solution)/shard_map/pgvj,pgij->pgvi/dot_general | solution.py:109
  (34 shorter events, 0.9 us)
Async XLA Ops:
  0.0 118.8 %copy-start = (bf16[1,8,384,384]{3,2,1,0:T(8,128)(2,1)S(1)}, bf16[1,8,384,384]{3,2,1,0:T(8,128)(2,1)}, u32[]{:S(2)}) copy-start(bf16[1,8,384,384]{3,2,1,0:T(8,128)(2,1)} %param.17) | copy-start | bytes 7077892
  0.0 25.8 %copy-start.1 = (f32[2,2,3,16,256]{4,3,2,1,0:T(8,128)S(1)}, f32[2,2,3,16,256]{4,3,2,1,0:T(8,128)}, u32[]{:S(2)}) copy-start(f32[2,2,3,16,256]{4,3,2,1,0:T(8,128)} %param.10) | copy-start | bytes 589828
  0.0 25.8 %copy-start.2 = (s32[8,256]{1,0:T(8,128)S(1)}, s32[8,256]{1,0:T(8,128)}, u32[]{:S(2)}) copy-start(s32[8,256]{1,0:T(8,128)} %param.12) | copy-start | bytes 24580
  0.0 26.5 %copy-start.3 = (f32[3,256]{1,0:T(4,128)S(1)}, f32[3,256]{1,0:T(4,128)}, u32[]{:S(2)}) copy-start(f32[3,256]{1,0:T(4,128)} %param.16) | copy-start | bytes 9220
  5.9 24.4 %collective-permute-start = (bf16[2,3,16,64]{3,2,1,0:T(8,128)(2,1)}, bf16[2,3,16,64]{3,2,1,0:T(8,128)(2,1)}, u32[]{:S(2)}, u32[]{:S(2)}) collective-permute-start(bf16[2,3,16,64]{3,2,1,0:T(8,128)(2,1)} %bitcast_convert_fusion.1), channel_id=1, source_target_pairs={{0,1},{2,3},{4,5},{6,7},{8,9},{10,11},{12,13},{14,15},{16,17},{18,... | collective-permute-start | bytes 36872 | tf_op jit(solution)/shard_map/ppermute | solution.py:24
  14.9 15.4 %collective-permute-start.1 = (bf16[2,3,16,64]{3,2,1,0:T(8,128)(2,1)}, bf16[2,3,16,64]{3,2,1,0:T(8,128)(2,1)}, u32[]{:S(2)}, u32[]{:S(2)}) collective-permute-start(bf16[2,3,16,64]{3,2,1,0:T(8,128)(2,1)} %bitcast_convert_fusion), channel_id=1, source_target_pairs={{1,0},{3,2},{5,4},{7,6},{9,8},{11,10},{13,12},{15,14},{17,16},{19,... | collective-permute-start | bytes 36872 | tf_op jit(solution)/shard_map/ppermute | solution.py:27
  22.0 9.2 %collective-permute-start.3 = (f32[3,16,64]{2,1,0:T(8,128)S(1)}, f32[3,16,64]{2,1,0:T(8,128)S(1)}, u32[]{:S(2)}, u32[]{:S(2)}) collective-permute-start(f32[3,16,64]{2,1,0:T(8,128)S(1)} %get-tuple-element.21), channel_id=1, source_target_pairs={{2,0},{4,2},{6,4},{8,6},{10,8},{12,10},{14,12},{16,14},{18,16},{20... | collective-permute-start | bytes 36872 | tf_op jit(solution)/shard_map/ppermute | solution.py:27
  25.8 5.9 %collective-permute-start.2 = (f32[3,16,64]{2,1,0:T(8,128)S(1)}, f32[3,16,64]{2,1,0:T(8,128)S(1)}, u32[]{:S(2)}, u32[]{:S(2)}) collective-permute-start(f32[3,16,64]{2,1,0:T(8,128)S(1)} %get-tuple-element.22), channel_id=1, source_target_pairs={{0,2},{2,4},{4,6},{6,8},{8,10},{10,12},{12,14},{14,16},{16,18},{18... | collective-permute-start | bytes 36872 | tf_op jit(solution)/shard_map/ppermute | solution.py:24
  76.6 14.3 %all-to-all-start = ((f32[16,1,3072]{2,1,0:T(1,128)}), f32[16,1,3072]{2,1,0:T(1,128)S(1)}, u32[]{:S(2)}, u32[]{:S(2)}) async-start(f32[16,1,3072]{2,1,0:T(1,128)} %reshape.174), calls=%async_computation | async-start | bytes 393216 | tf_op jit(solution)/shard_map/all_to_all | solution.py:98
where the time goes:
time: 121 us; the launch traced here: 120 us
  local copies, waits for them, and re-layouts  59 us (49%)
  starting transfers between devices  15.9 us (13%)
  matrix products  13.1 us (11%)
  other arithmetic  12.6 us (10%)
  blocking collectives  9.96 us (8%)
  waiting for transfers between devices  9.41 us (8%)
    gather x1, local copies, waits for them, and re-layouts, on_device(): picked = jnp.take(extended, neighbors, axis=3)  23.2 us
    unnamed x14, local copies, waits for them, and re-layouts  11.1 us
    dot_general x1, matrix products, on_device(): jnp.einsum('cdkn,sdvkn->scvn', stiffness, picked, precision=lax.Precision...  10.7 us
    all_to_all x1, blocking collectives, on_device(): lax.all_to_all(transformed, 'wheel', split_axis=0, concat_axis=4, tiled=T...  9.96 us
    all_to_all x1, waiting for transfers between devices, on_device(): lax.all_to_all(residual, 'wheel', split_axis=4, concat_axis=1, tiled=True)  8.93 us
    all_to_all x3, local copies, waits for them, and re-layouts, on_device(): lax.all_to_all(residual, 'wheel', split_axis=4, concat_axis=1, tiled=True)  6.2 us
    ppermute x2, starting transfers between devices, extended_2(): lax.ppermute(lax.slice_in_dim(block, block.shape[dim] - width, None, axis...  5.49 us
    all_to_all x1, starting transfers between devices, on_device(): lax.all_to_all(residual, 'wheel', split_axis=4, concat_axis=1, tiled=True)  5.36 us
  transfers between devices with their start and end apart: 5, of which 2 were waited for; matrix products, arithmetic and copies ran while one was open for 12% of the time, Pallas kernels for 0%

commit v1 on v0

v1 whole, which is shorter than its diff:
```python
import functools
import math

import jax
import jax.numpy as jnp
import numpy as np
from jax import lax
from jax.experimental import pallas as pl
from jax.experimental.pallas import tpu as pltpu
from jax.sharding import PartitionSpec as P

GROUP = 32
LANES = 128
COMPS = 3

damping_ratio = 0.5
gyro_rate = 0.8
shift_value = 0.3
class_step = 0.125

BF = jnp.bfloat16
F32 = jnp.float32


def basis(sectors_all):
    row = np.arange(sectors_all)[:, None]
    sector = np.arange(sectors_all)[None, :]
    pair, part = row // 2, row % 2
    angles = 2.0 * math.pi / sectors_all * (pair * sector % sectors_all)
    edge = np.where(part == 0, 1.0, 1.0 - 2.0 * (sector % 2)) * math.sqrt(1.0 / sectors_all)
    inner = np.where(part == 0, np.cos(angles), np.sin(angles)) * math.sqrt(2.0 / sectors_all)
    return np.where(pair == 0, edge, inner)


def selection(wheel, local, rows, fields):
    sectors = wheel * local
    out = np.zeros((len(fields), COMPS, sectors, wheel, rows), np.float32)
    for f, weights in enumerate(fields):
        for t, weight in enumerate(weights):
            for c in range(COMPS):
                for s in range(sectors):
                    out[f, c, s, s // local, (t * local + s % local) * COMPS + c] = weight
    return out.reshape(len(fields) * COMPS * sectors, wheel * rows)


def scale_selection(wheel, local, rows):
    sectors = wheel * local
    out = np.zeros((sectors, wheel, rows), np.float32)
    for s in range(sectors):
        out[s, s // local, 2 * local * COMPS + s % local] = 1.0
    return out.reshape(sectors, wheel * rows)


def transform(sectors):
    table = basis(sectors).reshape(sectors // 2, 2, sectors)
    out = np.zeros((2, 2, COMPS, sectors // 2, 2, COMPS, sectors), np.float32)
    for t in range(2):
        for c in range(COMPS):
            out[:, t, c, :, t, c, :] = table.transpose(1, 0, 2)
    return out.reshape(2 * 2 * COMPS * (sectors // 2), 2 * COMPS * sectors)


def split(x):
    high = x.astype(BF)
    return high, (x - high.astype(F32)).astype(BF)


def dot(a, b):
    return jnp.dot(a, b, preferred_element_type=F32)


def pack_body(vecs, local, copies, krylov, blade, iface, out, rows, sems):
    halves = rows.shape[0]
    data = krylov.shape[0]
    moves = [
        pltpu.make_async_copy(
            krylov.at[:, pl.ds(h * LANES, LANES)], rows.at[h, pl.ds(0, data)], sems.at[h]
        )
        for h in range(halves)
    ]
    for move in moves:
        move.start()
    width = iface.shape[1]
    for h in range(halves):
        at = data
        for l in range(local):
            scale = 1.0 + class_step * blade[l].astype(F32)
            rows[h, at : at + vecs, :] = jnp.full((vecs, LANES), scale, F32)
            at += vecs
        for side in range(2):
            rows[h, at : at + vecs, :] = jnp.zeros((vecs, LANES), F32)
            if h == 0:
                rows[h, at : at + vecs, 0:width] = jnp.broadcast_to(
                    iface[side : side + 1, :].astype(F32), (vecs, width)
                )
            at += vecs
    for h, move in enumerate(moves):
        move.wait()
        for v in range(vecs):
            chunk = rows[h, pl.ds(v, rows.shape[1] // vecs, stride=vecs), :].astype(BF)
            for i in range(copies):
                out[v * copies + i, :, h * LANES : (h + 1) * LANES] = chunk


def tables_body(neighbors, faces, onehot, pick):
    count, nodes = neighbors.shape
    extended = onehot.shape[0]
    index = lax.broadcasted_iota(jnp.int32, (extended, nodes), 0)
    for k in range(count):
        hit = index == neighbors[k : k + 1, :]
        onehot[:, k * nodes : (k + 1) * nodes] = jnp.where(hit, 1.0, 0.0).astype(BF)
    width = faces.shape[1]
    index = lax.broadcasted_iota(jnp.int32, (nodes, width), 0)
    for i, side in enumerate((1, 0)):
        hit = index == faces[side : side + 1, :]
        pick[:, i * width : (i + 1) * width] = jnp.where(hit, 1.0, 0.0).astype(BF)


def residual_body(
    slabs, wheel, local, width, x, *refs
):
    lows = refs[: len(refs) - 11]
    onehot, pick, stiffness, mass, sel, sel_scale, sel_moved, table, out, rim, rows = refs[-11:]
    nodes = x.shape[-1]
    sectors = wheel * local
    count = stiffness.shape[2]
    slab = lax.axis_index("slab")
    height = x.shape[-2]
    extras = 2 * local * COMPS + local
    if slabs == 2:
        own = x[:, pl.ds(slab, 1)].reshape(wheel * height, nodes)
        sides = (x[:, pl.ds(1 - slab, 1)].reshape(wheel * height, nodes),)
    else:
        own = x[...].reshape(wheel * height, nodes)
        sides = tuple(ref[...].reshape(wheel * height, nodes) for ref in lows)

    uv = dot(sel[...], own)
    block = COMPS * sectors
    u, v = uv[:block], uv[block : 2 * block]
    scale = dot(sel_scale[...], own)
    moved = jnp.concatenate(split(u + damping_ratio * v), axis=0)

    index = lax.broadcasted_iota(jnp.int32, (nodes, width), 0)
    for i in range(2):
        side = sides[i % len(sides)]
        row = extras + 1 - i
        names = side[row : row + 1, 0:width].astype(F32).astype(jnp.int32)
        valid = (slab > 0) if i == 0 else (slab < slabs - 1)
        hit = (index == names) & valid
        rim[:, i * width : (i + 1) * width] = jnp.where(hit, 1.0, 0.0).astype(BF)
    if len(sides) == 1:
        other = jnp.concatenate(split(dot(sel_moved[...], sides[0])), axis=0)
        rims = dot(other, rim[...])
    else:
        parts = [
            dot(jnp.concatenate(split(dot(sel_moved[...], side)), axis=0), rim[...])
            for side in sides
        ]
        lane = lax.broadcasted_iota(jnp.int32, parts[0].shape, 1)
        rims = jnp.where(lane < width, parts[0], parts[1])

    faces = dot(moved, pick[...])
    turned = []
    for i in range(2 * COMPS):
        part = faces[i * sectors : (i + 1) * sectors]
        lane = lax.broadcasted_iota(jnp.int32, part.shape, 1)
        before = pltpu.roll(part, 1, axis=0)
        after = pltpu.roll(part, sectors - 1, axis=0)
        turned.append(jnp.where(lane < width, before, after))
    extended = jnp.concatenate(
        (moved, rims.astype(BF), jnp.concatenate(turned, axis=0).astype(BF)), axis=1
    )

    restore = [None] * COMPS
    for k in range(count):
        picked = dot(extended, onehot[:, k * nodes : (k + 1) * nodes])
        picked = picked[:block] + picked[block:]
        for d in range(COMPS):
            term = picked[d * sectors : (d + 1) * sectors]
            for c in range(COMPS):
                part = stiffness[c, d, k : k + 1, :] * term
                restore[c] = part if restore[c] is None else restore[c] + part

    vc = [v[c * sectors : (c + 1) * sectors] for c in range(COMPS)]
    lumped = [mass[c : c + 1, :] for c in range(COMPS)]
    gyro = (-(gyro_rate * lumped[0]) * vc[1], (gyro_rate * lumped[1]) * vc[0], None)
    residual = [v - shift_value * u]
    for c in range(COMPS):
        part = -scale * restore[c] - (shift_value * lumped[c]) * vc[c]
        residual.append(part if gyro[c] is None else part - gyro[c])
    high, low = split(jnp.concatenate(residual, axis=0))
    harmonic = dot(table[...], jnp.concatenate((high, low, high), axis=0))
    halves = nodes // LANES
    kinds = 4 * COMPS
    pairs = sectors // 2
    for h in range(halves):
        for r in range(kinds):
            rows[pl.ds(h * kinds + r, pairs, stride=halves * kinds), :] = harmonic[
                r * pairs : (r + 1) * pairs, h * LANES : (h + 1) * LANES
            ]
    out[...] = rows[...].astype(BF).reshape(out.shape)


def apply_body(vecs, spread, y, precond, out, rows):
    kinds = 4 * COMPS
    per = LANES // GROUP
    chunk = y.shape[1]
    halves = chunk // kinds
    rows[...] = y[...].astype(F32).reshape(rows.shape)
    lane = lax.broadcasted_iota(jnp.int32, (vecs, LANES), 1)
    for h in range(halves):
        tiles = [[] for _ in range(per)]
        for j in range(kinds // per):
            blocks = [
                rows[pl.ds(h * kinds + j * per + r, vecs, stride=chunk * spread), :]
                for r in range(per)
            ]
            step = per // 2
            while step:
                shift = step * GROUP
                upper = (lane // shift) % 2 == 1
                fresh = list(blocks)
                for r in range(per):
                    if r & step == 0:
                        a, b = blocks[r], blocks[r + step]
                        fresh[r] = jnp.where(upper, pltpu.roll(b, shift, axis=1), a)
                        fresh[r + step] = jnp.where(
                            upper, b, pltpu.roll(a, LANES - shift, axis=1)
                        )
                blocks = fresh
                step //= 2
            for g in range(per):
                tiles[g].append(blocks[g].astype(BF))
        for g in range(per):
            lhs = jnp.concatenate(tiles[g], axis=1)
            out[h * per + g] = lax.dot_general(
                lhs,
                precond[h * per + g],
                (((1,), (1,)), ((), ())),
                preferred_element_type=F32,
            )


def on_device(
    wheel, slabs, krylov_block, blade_class, neighbors, iface_rows, face_rows, stiffness, lumped_mass, precond
):
    states, local, comps, vecs, nodes = krylov_block.shape
    width = iface_rows.shape[1]
    spread = wheel // vecs
    sectors = wheel * local
    height = 2 * local * comps + local + 2
    count = neighbors.shape[0]
    extended = nodes + 4 * width
    vmem = pl.BlockSpec(memory_space=pltpu.VMEM)
    smem = pl.BlockSpec(memory_space=pltpu.SMEM)
    anywhere = pl.BlockSpec(memory_space=pl.ANY)

    fan = slabs if slabs == 2 else 1
    packed = pl.pallas_call(
        functools.partial(pack_body, vecs, local, spread * fan),
        out_shape=jax.ShapeDtypeStruct((wheel * fan, height, nodes), BF),
        in_specs=[anywhere, smem, vmem],
        out_specs=vmem,
        scratch_shapes=[
            pltpu.VMEM((nodes // LANES, height * vecs, LANES), F32),
            pltpu.SemaphoreType.DMA((nodes // LANES,)),
        ],
    )(krylov_block.reshape(states * local * comps * vecs, nodes), blade_class, iface_rows)
    onehot, pick = pl.pallas_call(
        tables_body,
        out_shape=(
            jax.ShapeDtypeStruct((extended, count * nodes), BF),
            jax.ShapeDtypeStruct((nodes, 2 * width), BF),
        ),
        in_specs=[vmem, vmem],
        out_specs=(vmem, vmem),
    )(neighbors, face_rows)
    if slabs == 2:
        got = lax.all_to_all(packed, ("wheel", "slab"), 0, 0, tiled=True)
        got = got.reshape(wheel, slabs, height, nodes)
        sides = ()
    else:
        got = lax.all_to_all(packed, "wheel", 0, 0, tiled=True)
        up = [(i, i + 1) for i in range(slabs - 1)]
        down = [(i + 1, i) for i in range(slabs - 1)]
        sides = (lax.ppermute(got, "slab", up), lax.ppermute(got, "slab", down))

    sel = selection(wheel, local, height, ((1.0, 0.0), (0.0, 1.0)))
    sel_moved = selection(wheel, local, height, ((1.0, damping_ratio),))
    sel_scale = scale_selection(wheel, local, height)
    table = transform(sectors)
    high = table.astype(jnp.bfloat16)
    low = (table - high.astype(np.float32)).astype(jnp.bfloat16)
    table = np.concatenate((high, high, low), axis=1)
    kinds = 4 * comps
    pairs = sectors // 2
    chunk = kinds * (nodes // LANES)
    sent = pl.pallas_call(
        functools.partial(residual_body, slabs, wheel, local, width),
        out_shape=jax.ShapeDtypeStruct((pairs, chunk, LANES), BF),
        in_specs=[vmem] * (9 + len(sides)),
        out_specs=vmem,
        scratch_shapes=[
            pltpu.VMEM((nodes, 2 * width), BF),
            pltpu.VMEM((pairs * chunk, LANES), F32),
        ],
    )(
        got,
        *sides,
        onehot,
        pick,
        stiffness,
        lumped_mass,
        jnp.asarray(sel, BF),
        jnp.asarray(sel_scale, BF),
        jnp.asarray(sel_moved, BF),
        jnp.asarray(table),
    )
    back = lax.all_to_all(sent, "wheel", 0, 0, tiled=True)
    owned, groups, order, _ = precond.shape
    out = pl.pallas_call(
        functools.partial(apply_body, vecs, spread),
        out_shape=jax.ShapeDtypeStruct((groups, vecs, order), F32),
        in_specs=[vmem, vmem],
        out_specs=vmem,
        scratch_shapes=[pltpu.VMEM((wheel * chunk, LANES), F32)],
    )(back, precond.reshape(groups, order, order))
    return out.reshape(owned, groups, vecs, order)


def solution(mesh):
    return jax.shard_map(
        functools.partial(on_device, mesh.shape["wheel"], mesh.shape["slab"]),
        mesh=mesh,
        in_specs=(
            P(None, "wheel", None, None, "slab"),
            P("wheel"),
            P(None, "slab"),
            P(None, "slab"),
            P(None, "slab"),
            P(None, None, None, "slab"),
            P(None, "slab"),
            P("wheel", "slab", None, None),
        ),
        out_specs=P("wheel", "slab", None, None),
        check_vma=False,
    )
```

time: 121 us -> 40 us (0.33)
  local copies, waits for them, and re-layouts: 59 us -> 0.72 us
  matrix products: 13.1 us -> 0 us
  other arithmetic: 12.6 us -> 0 us
  Pallas kernels: 0 us -> 12 us
  starting transfers between devices: 15.9 us -> 7.33 us
  blocking collectives: 9.96 us -> 11.5 us
  waiting for transfers between devices: 9.41 us -> 7.99 us
    gather x9 -> x0, local copies, waits for them, and re-layouts: 31.2 us -> none  [the longest x1 23.2 us: on_device(): picked = jnp.take(extended, neighbors, axis=3)]
    dot_general x2 -> x0, matrix products: 12.2 us -> none  [the longest x1 10.7 us: on_device(): jnp.einsum('cdkn,sdvkn->scvn', stiffness, picked, precision=lax.Precision...]
    pallas_call x0 -> x4, Pallas kernels: none -> 12 us  [the longest x1 3.62 us: on_device(): pl.pallas_call(functools.partial(residual_body, slabs, wheel, local, widt...]
    ppermute x4 -> x0, starting transfers between devices: 10.5 us -> none  [the longest x2 5.49 us: extended_2(): lax.ppermute(lax.slice_in_dim(block, block.shape[dim] - width, None, axis...]
    unnamed x14 -> x2, local copies, waits for them, and re-layouts: 11.1 us -> 0.72 us
    all_to_all x4 -> x0, local copies, waits for them, and re-layouts: 7.6 us -> none  [the longest x3 6.2 us: on_device(): lax.all_to_all(residual, 'wheel', split_axis=4, concat_axis=1, tiled=True)]
    slice x2 -> x0, other arithmetic: 2.7 us -> none  [the longest x1 1.35 us: extended_2(): lax.slice_in_dim(block, block.shape[dim] - width, None, axis=dim)]
    another operation x3 -> x0, local copies, waits for them, and re-layouts: 2.56 us -> none  [the longest x1 2.16 us: on_device(): residual = jnp.stack((res_disp, res_velo), axis=0)]
  transfers between devices with their start and end apart: 5 -> 1, of which waited for: 2 -> 1; matrix products, arithmetic and copies ran while one was open for 12% -> 0% of each run, Pallas kernels for 0% -> 7%
where the time goes in v1:
time: 40 us; the launch traced here: 39.6 us
  Pallas kernels  12 us (30%)
  blocking collectives  11.5 us (29%)
  waiting for transfers between devices  7.99 us (20%)
  starting transfers between devices  7.33 us (18%)
  local copies, waits for them, and re-layouts  0.72 us (2%)
    all_to_all x1, blocking collectives, on_device(): back = lax.all_to_all(sent, 'wheel', 0, 0, tiled=True)  11.5 us
    all_to_all x1, waiting for transfers between devices, on_device(): got = lax.all_to_all(packed, ('wheel', 'slab'), 0, 0, tiled=True)  7.99 us
    all_to_all x1, starting transfers between devices, on_device(): got = lax.all_to_all(packed, ('wheel', 'slab'), 0, 0, tiled=True)  7.33 us
    pallas_call x1, Pallas kernels, on_device(): pl.pallas_call(functools.partial(residual_body, slabs, wheel, local, widt...  3.62 us
    pallas_call x1, Pallas kernels, on_device(): pl.pallas_call(functools.partial(apply_body, vecs, spread), out_shape=jax...  3.32 us
    pallas_call x1, Pallas kernels, on_device(): pl.pallas_call(tables_body, out_shape=(jax.ShapeDtypeStruct((extended, co...  2.67 us
    pallas_call x1, Pallas kernels, on_device(): pl.pallas_call(functools.partial(pack_body, vecs, local, spread * fan), o...  2.42 us
  transfers between devices with their start and end apart: 1, of which 1 were waited for; matrix products, arithmetic and copies ran while one was open for 0% of the time, Pallas kernels for 7%

profile of v1, /device:TPU:0, one launch (start us, length us, event | category | flops | bytes accessed | tf_op | source)
XLA Modules:
  0.0 39.6 jit_solution(11815599377076018210)
XLA Ops:
  0.0 2.4 %shard_map.118 = bf16[32,16,256]{2,1,0:T(8,128)(2,1)} custom-call(f32[192,256]{1,0:T(8,128)} %bitcast.6, s32[2]{0:T(128)} %blade.1, s32[2,64]{1,0:T(2,128)} %iface.1), custom_call_target="tpu_custom_call" | custom-call | tf_op jit(solution)/shard_map/pallas_call | solution.py:259
  2.4 7.3 %all-to-all-start = ((bf16[32,16,256]{2,1,0:T(8,128)(2,1)}), bf16[32,16,256]{2,1,0:T(8,128)(2,1)S(1)}, u32[]{:S(2)}, u32[]{:S(2)}) async-start(bf16[32,16,256]{2,1,0:T(8,128)(2,1)} %shard_map.118), calls=%async_computation | async-start | bytes 524288 | tf_op jit(solution)/shard_map/all_to_all | solution.py:279
  9.8 2.7 %shard_map.119 = (bf16[512,2048]{1,0:T(8,128)(2,1)}, bf16[256,128]{1,0:T(8,128)(2,1)}) custom-call(s32[8,256]{1,0:T(8,128)} %neighbors.1, s32[2,64]{1,0:T(2,128)} %faces.1), custom_call_target="tpu_custom_call" | custom-call | tf_op jit(solution)/shard_map/pallas_call | solution.py:269
  12.4 8.0 %all-to-all-done = bf16[32,16,256]{2,1,0:T(8,128)(2,1)S(1)} async-done(((bf16[32,16,256]{2,1,0:T(8,128)(2,1)}), bf16[32,16,256]{2,1,0:T(8,128)(2,1)S(1)}, u32[]{:S(2)}, u32[]{:S(2)}) %all-to-all-start) | async-done | bytes 262176 | tf_op jit(solution)/shard_map/all_to_all | solution.py:279
  20.4 0.0 copy-start
  20.4 0.7 %copy-done = bf16[32,16,256]{2,1,0:T(8,128)(2,1)} copy-done((bf16[32,16,256]{2,1,0:T(8,128)(2,1)}, bf16[32,16,256]{2,1,0:T(8,128)(2,1)S(1)}, u32[]{:S(2)}) %copy-start) | copy-done | bytes 262168
  21.2 3.6 %shard_map.120 = bf16[16,24,128]{2,1,0:T(8,128)(2,1)} custom-call(bf16[16,2,16,256]{3,2,1,0:T(8,128)(2,1)} %bitcast.5, bf16[512,2048]{1,0:T(8,128)(2,1)} %get-tuple-element.7.refs_0_, bf16[256,128]{1,0:T(8,128)(2,1)} %get-tuple-element.8.refs_1_, f32[3,3,8,256]{3,2,1,0:T(8,128)} %refs_2_.1, f32[3,256]{1,0:T(4,128)} %refs_3_.1, ...), custom_call_target="tpu_custom_call" | custom-call | tf_op jit(solution)/shard_map/pallas_call | solution.py:298
  24.8 11.5 %all_to_all.10.y = bf16[16,24,128]{2,1,0:T(8,128)(2,1)} all-to-all(bf16[16,24,128]{2,1,0:T(8,128)(2,1)} %shard_map.120), channel_id=1, replica_groups=mesh['wheel'=16,'slab'=2] {'wheel'}, dimensions={0} | all-to-all | bytes 196608 | tf_op jit(solution)/shard_map/all_to_all | solution.py:319
  36.3 3.3 %shard_map.121 = f32[8,16,384]{2,1,0:T(8,128)} custom-call(bf16[16,24,128]{2,1,0:T(8,128)(2,1)} %all_to_all.10.y, bf16[8,384,384]{2,1,0:T(8,128)(2,1)} %bitcast.4), custom_call_target="tpu_custom_call" | custom-call | tf_op jit(solution)/shard_map/pallas_call | solution.py:321
Async XLA Ops:
  2.4 18.0 %all-to-all-start = ((bf16[32,16,256]{2,1,0:T(8,128)(2,1)}), bf16[32,16,256]{2,1,0:T(8,128)(2,1)S(1)}, u32[]{:S(2)}, u32[]{:S(2)}) async-start(bf16[32,16,256]{2,1,0:T(8,128)(2,1)} %shard_map.118), calls=%async_computation | async-start | bytes 524288 | tf_op jit(solution)/shard_map/all_to_all | solution.py:279
  20.4 0.7 %copy-start = (bf16[32,16,256]{2,1,0:T(8,128)(2,1)}, bf16[32,16,256]{2,1,0:T(8,128)(2,1)S(1)}, u32[]{:S(2)}) copy-start(bf16[32,16,256]{2,1,0:T(8,128)(2,1)S(1)} %all-to-all-done) | copy-start | bytes 786436

commit v2 on v1

--- a/solution.py
+++ b/solution.py
@@ -20,6 +20,15 @@
 
 BF = jnp.bfloat16
 F32 = jnp.float32
+LIMIT = 16 << 20
+
+
+def hold(x):
+    return pltpu.with_memory_space_constraint(x, pltpu.HBM)
+
+
+def near(x):
+    return pltpu.with_memory_space_constraint(x, pltpu.VMEM)
 
 
 def basis(sectors_all):
@@ -69,7 +78,10 @@
     return jnp.dot(a, b, preferred_element_type=F32)
 
 
-def pack_body(vecs, local, copies, krylov, blade, iface, out, rows, sems):
+def pack_body(vecs, local, copies, krylov, blade, iface, faces, *refs):
+    kept = (len(refs) - 7) // 2
+    sources, out, pick, targets = refs[:kept], refs[kept], refs[kept + 1], refs[kept + 2 : 2 * kept + 2]
+    rows, classes, names, sides, sems = refs[-5:]
     halves = rows.shape[0]
     data = krylov.shape[0]
     moves = [
@@ -78,20 +90,34 @@
         )
         for h in range(halves)
     ]
-    for move in moves:
+    small = [
+        pltpu.make_async_copy(source, target, sems.at[halves + i])
+        for i, (source, target) in enumerate(((blade, classes), (iface, names), (faces, sides)))
+    ]
+    rest = [
+        pltpu.make_async_copy(source, target, sems.at[halves + 3 + i])
+        for i, (source, target) in enumerate(zip(sources, targets))
+    ]
+    for move in small + moves + rest:
         move.start()
-    width = iface.shape[1]
+    for move in small:
+        move.wait()
+    width = names.shape[1]
+    index = lax.broadcasted_iota(jnp.int32, (pick.shape[0], width), 0)
+    for i, side in enumerate((1, 0)):
+        hit = index == sides[side : side + 1, :]
+        pick[:, i * width : (i + 1) * width] = jnp.where(hit, 1.0, 0.0).astype(BF)
     for h in range(halves):
         at = data
         for l in range(local):
-            scale = 1.0 + class_step * blade[l].astype(F32)
+            scale = 1.0 + class_step * classes[l].astype(F32)
             rows[h, at : at + vecs, :] = jnp.full((vecs, LANES), scale, F32)
             at += vecs
         for side in range(2):
             rows[h, at : at + vecs, :] = jnp.zeros((vecs, LANES), F32)
             if h == 0:
                 rows[h, at : at + vecs, 0:width] = jnp.broadcast_to(
-                    iface[side : side + 1, :].astype(F32), (vecs, width)
+                    names[side : side + 1, :].astype(F32), (vecs, width)
                 )
             at += vecs
     for h, move in enumerate(moves):
@@ -100,27 +126,16 @@
             chunk = rows[h, pl.ds(v, rows.shape[1] // vecs, stride=vecs), :].astype(BF)
             for i in range(copies):
                 out[v * copies + i, :, h * LANES : (h + 1) * LANES] = chunk
-
-
-def tables_body(neighbors, faces, onehot, pick):
-    count, nodes = neighbors.shape
-    extended = onehot.shape[0]
-    index = lax.broadcasted_iota(jnp.int32, (extended, nodes), 0)
-    for k in range(count):
-        hit = index == neighbors[k : k + 1, :]
-        onehot[:, k * nodes : (k + 1) * nodes] = jnp.where(hit, 1.0, 0.0).astype(BF)
-    width = faces.shape[1]
-    index = lax.broadcasted_iota(jnp.int32, (nodes, width), 0)
-    for i, side in enumerate((1, 0)):
-        hit = index == faces[side : side + 1, :]
-        pick[:, i * width : (i + 1) * width] = jnp.where(hit, 1.0, 0.0).astype(BF)
+    for move in rest:
+        move.wait()
 
 
 def residual_body(
     slabs, wheel, local, width, x, *refs
 ):
-    lows = refs[: len(refs) - 11]
-    onehot, pick, stiffness, mass, sel, sel_scale, sel_moved, table, out, rim, rows = refs[-11:]
+    ins, (out, rim, rows) = refs[:-3], refs[-3:]
+    lows = ins[: 0 if slabs == 2 else 2]
+    pick, neighbors, stiffness, mass, sel, sel_scale, sel_moved, table = ins[len(lows) :]
     nodes = x.shape[-1]
     sectors = wheel * local
     count = stiffness.shape[2]
@@ -172,8 +187,10 @@
     )
 
     restore = [None] * COMPS
+    index = lax.broadcasted_iota(jnp.int32, (extended.shape[1], nodes), 0)
     for k in range(count):
-        picked = dot(extended, onehot[:, k * nodes : (k + 1) * nodes])
+        hit = index == neighbors[k : k + 1, :]
+        picked = dot(extended, jnp.where(hit, 1.0, 0.0).astype(BF))
         picked = picked[:block] + picked[block:]
         for d in range(COMPS):
             term = picked[d * sectors : (d + 1) * sectors]
@@ -249,32 +266,50 @@
     spread = wheel // vecs
     sectors = wheel * local
     height = 2 * local * comps + local + 2
-    count = neighbors.shape[0]
-    extended = nodes + 4 * width
     vmem = pl.BlockSpec(memory_space=pltpu.VMEM)
-    smem = pl.BlockSpec(memory_space=pltpu.SMEM)
     anywhere = pl.BlockSpec(memory_space=pl.ANY)
 
+    sel = selection(wheel, local, height, ((1.0, 0.0), (0.0, 1.0)))
+    sel_moved = selection(wheel, local, height, ((1.0, damping_ratio),))
+    sel_scale = scale_selection(wheel, local, height)
+    table = transform(sectors)
+    high = table.astype(jnp.bfloat16)
+    low = (table - high.astype(np.float32)).astype(jnp.bfloat16)
+    table = np.concatenate((high, high, low), axis=1)
+    kept = (
+        neighbors,
+        stiffness,
+        lumped_mass,
+        jnp.asarray(sel, BF),
+        jnp.asarray(sel_scale, BF),
+        jnp.asarray(sel_moved, BF),
+        jnp.asarray(table),
+    )
     fan = slabs if slabs == 2 else 1
-    packed = pl.pallas_call(
+    packed, *tables = pl.pallas_call(
         functools.partial(pack_body, vecs, local, spread * fan),
-        out_shape=jax.ShapeDtypeStruct((wheel * fan, height, nodes), BF),
-        in_specs=[anywhere, smem, vmem],
-        out_specs=vmem,
+        out_shape=(
+            pltpu.VMEM((wheel * fan, height, nodes), BF),
+            pltpu.VMEM((nodes, 2 * width), BF),
+            *(pltpu.VMEM(x.shape, x.dtype) for x in kept),
+        ),
+        in_specs=[anywhere] * (4 + len(kept)),
+        out_specs=(vmem,) * (2 + len(kept)),
         scratch_shapes=[
             pltpu.VMEM((nodes // LANES, height * vecs, LANES), F32),
-            pltpu.SemaphoreType.DMA((nodes // LANES,)),
+            pltpu.SMEM(blade_class.shape, jnp.int32),
+            pltpu.VMEM(iface_rows.shape, jnp.int32),
+            pltpu.VMEM(face_rows.shape, jnp.int32),
+            pltpu.SemaphoreType.DMA((nodes // LANES + 3 + len(kept),)),
         ],
-    )(krylov_block.reshape(states * local * comps * vecs, nodes), blade_class, iface_rows)
-    onehot, pick = pl.pallas_call(
-        tables_body,
-        out_shape=(
-            jax.ShapeDtypeStruct((extended, count * nodes), BF),
-            jax.ShapeDtypeStruct((nodes, 2 * width), BF),
-        ),
-        in_specs=[vmem, vmem],
-        out_specs=(vmem, vmem),
-    )(neighbors, face_rows)
+        compiler_params=pltpu.CompilerParams(vmem_limit_bytes=LIMIT),
+    )(
+        hold(krylov_block.reshape(states * local * comps * vecs, nodes)),
+        hold(blade_class),
+        hold(iface_rows),
+        hold(face_rows),
+        *(hold(x) for x in kept),
+    )
     if slabs == 2:
         got = lax.all_to_all(packed, ("wheel", "slab"), 0, 0, tiled=True)
         got = got.reshape(wheel, slabs, height, nodes)
@@ -285,37 +320,20 @@
         down = [(i + 1, i) for i in range(slabs - 1)]
         sides = (lax.ppermute(got, "slab", up), lax.ppermute(got, "slab", down))
 
-    sel = selection(wheel, local, height, ((1.0, 0.0), (0.0, 1.0)))
-    sel_moved = selection(wheel, local, height, ((1.0, damping_ratio),))
-    sel_scale = scale_selection(wheel, local, height)
-    table = transform(sectors)
-    high = table.astype(jnp.bfloat16)
-    low = (table - high.astype(np.float32)).astype(jnp.bfloat16)
-    table = np.concatenate((high, high, low), axis=1)
     kinds = 4 * comps
     pairs = sectors // 2
     chunk = kinds * (nodes // LANES)
     sent = pl.pallas_call(
         functools.partial(residual_body, slabs, wheel, local, width),
-        out_shape=jax.ShapeDtypeStruct((pairs, chunk, LANES), BF),
-        in_specs=[vmem] * (9 + len(sides)),
+        out_shape=pltpu.VMEM((pairs, chunk, LANES), BF),
+        in_specs=[vmem] * (1 + len(sides) + len(tables)),
         out_specs=vmem,
         scratch_shapes=[
             pltpu.VMEM((nodes, 2 * width), BF),
             pltpu.VMEM((pairs * chunk, LANES), F32),
         ],
-    )(
-        got,
-        *sides,
-        onehot,
-        pick,
-        stiffness,
-        lumped_mass,
-        jnp.asarray(sel, BF),
-        jnp.asarray(sel_scale, BF),
-        jnp.asarray(sel_moved, BF),
-        jnp.asarray(table),
-    )
+        compiler_params=pltpu.CompilerParams(vmem_limit_bytes=LIMIT),
+    )(near(got), *(near(x) for x in sides), *(near(x) for x in tables))
     back = lax.all_to_all(sent, "wheel", 0, 0, tiled=True)
     owned, groups, order, _ = precond.shape
     out = pl.pallas_call(
@@ -324,7 +342,8 @@
         in_specs=[vmem, vmem],
         out_specs=vmem,
         scratch_shapes=[pltpu.VMEM((wheel * chunk, LANES), F32)],
-    )(back, precond.reshape(groups, order, order))
+        compiler_params=pltpu.CompilerParams(vmem_limit_bytes=LIMIT),
+    )(near(back), near(precond.reshape(groups, order, order)))
     return out.reshape(owned, groups, vecs, order)
 
 

time: 40 us -> 32.3 us (0.81)
  blocking collectives: 11.5 us -> 27.8 us
  waiting for transfers between devices: 7.99 us -> 0 us
  Pallas kernels: 12 us -> 4.36 us
  starting transfers between devices: 7.33 us -> 0 us
  local copies, waits for them, and re-layouts: 0.72 us -> 0.01 us
    all_to_all x0 -> x1, blocking collectives: none -> 17.8 us  [on_device(): got = lax.all_to_all(packed, ('wheel', 'slab'), 0, 0, tiled=True)]
    all_to_all x1 -> x0, waiting for transfers between devices: 7.99 us -> none  [on_device(): got = lax.all_to_all(packed, ('wheel', 'slab'), 0, 0, tiled=True)]
    all_to_all x1 -> x0, starting transfers between devices: 7.33 us -> none  [on_device(): got = lax.all_to_all(packed, ('wheel', 'slab'), 0, 0, tiled=True)]
    pallas_call x1 -> x0, Pallas kernels: 2.67 us -> none  [on_device(): pl.pallas_call(tables_body, out_shape=(jax.ShapeDtypeStruct((extended, co...]
    pallas_call x1, Pallas kernels: 3.62 us -> 1.29 us  [on_device(): pl.pallas_call(functools.partial(residual_body, slabs, wheel, local, widt...]
    pallas_call x1, Pallas kernels: 3.32 us -> 1.6 us  [on_device(): pl.pallas_call(functools.partial(apply_body, vecs, spread), out_shape=jax...]
    all_to_all x1, blocking collectives: 11.5 us -> 9.96 us  [on_device(): back = lax.all_to_all(sent, 'wheel', 0, 0, tiled=True)]
    pallas_call x1, Pallas kernels: 2.42 us -> 1.47 us  [on_device(): pl.pallas_call(functools.partial(pack_body, vecs, local, spread * fan), o...]
  transfers between devices with their start and end apart: 1 -> 0, of which waited for: 1 -> 0; matrix products, arithmetic and copies ran while one was open for 0% -> 0% of each run, Pallas kernels for 7% -> 0%
where the time goes in v2:
time: 32.3 us; the launch traced here: 32.1 us
  blocking collectives  27.8 us (86%)
  Pallas kernels  4.36 us (13%)
    all_to_all x1, blocking collectives, on_device(): got = lax.all_to_all(packed, ('wheel', 'slab'), 0, 0, tiled=True)  17.8 us
    all_to_all x1, blocking collectives, on_device(): back = lax.all_to_all(sent, 'wheel', 0, 0, tiled=True)  9.96 us
    pallas_call x1, Pallas kernels, on_device(): pl.pallas_call(functools.partial(apply_body, vecs, spread), out_shape=jax...  1.6 us
    pallas_call x1, Pallas kernels, on_device(): pl.pallas_call(functools.partial(pack_body, vecs, local, spread * fan), o...  1.47 us
    pallas_call x1, Pallas kernels, on_device(): pl.pallas_call(functools.partial(residual_body, slabs, wheel, local, widt...  1.29 us

profile of v2, /device:TPU:0, one launch (start us, length us, event | category | flops | bytes accessed | tf_op | source)
XLA Modules:
  0.0 32.1 jit_solution(6367925211460943853)
XLA Ops:
  0.0 0.0 copy-start
  0.0 1.5 %shard_map.118 = (bf16[32,16,256]{2,1,0:T(8,128)(2,1)S(1)}, bf16[256,128]{1,0:T(8,128)(2,1)S(1)}, s32[8,256]{1,0:T(8,128)S(1)}, f32[3,3,8,256]{3,2,1,0:T(8,128)S...) custom-call(f32[192,256]{1,0:T(8,128)} %bitcast.6, ...), custom_call_target="tpu_custom_call" | custom-call | tf_op jit(solution)/shard_map/pallas_call | solution.py:289
  1.5 17.8 %all_to_all.10 = bf16[32,16,256]{2,1,0:T(8,128)(2,1)S(1)} all-to-all(bf16[32,16,256]{2,1,0:T(8,128)(2,1)S(1)} %get-tuple-element.14), channel_id=1, replica_groups=mesh['wheel'=16,'slab'=2] {'wheel','slab'}, dimensions={0} | all-to-all | bytes 524288 | tf_op jit(solution)/shard_map/all_to_all | solution.py:314
  19.3 1.3 %shard_map.119 = bf16[16,24,128]{2,1,0:T(8,128)(2,1)S(1)} custom-call(bf16[16,2,16,256]{3,2,1,0:T(8,128)(2,1)S(1)} %bitcast.5, bf16[256,128]{1,0:T(8,128)(2,1)S(1)} %get-tuple-element.15.refs_0_, s32[8,256]{1,0:T(8,128)S(1)} %get-tuple-element.16.refs_1_, f32[3,3,8,256]{3,2,1,0:T(8,128)S(1)} %get-tuple-element.17.refs_2_, ...), custom_call_target="tpu_custom_call" | custom-call | tf_op jit(solution)/shard_map/pallas_call | solution.py:326
  20.6 10.0 %all_to_all.11.y = bf16[16,24,128]{2,1,0:T(8,128)(2,1)S(1)} all-to-all(bf16[16,24,128]{2,1,0:T(8,128)(2,1)S(1)} %shard_map.119), channel_id=1, replica_groups=mesh['wheel'=16,'slab'=2] {'wheel'}, dimensions={0} | all-to-all | bytes 196608 | tf_op jit(solution)/shard_map/all_to_all | solution.py:337
  30.5 0.0 copy-done
  30.5 1.6 %shard_map.120 = f32[8,16,384]{2,1,0:T(8,128)} custom-call(bf16[16,24,128]{2,1,0:T(8,128)(2,1)S(1)} %all_to_all.11.y, bf16[8,384,384]{2,1,0:T(8,128)(2,1)S(1)} %bitcast.4), custom_call_target="tpu_custom_call" | custom-call | tf_op jit(solution)/shard_map/pallas_call | solution.py:339
Async XLA Ops:
  0.0 30.5 %copy-start = (bf16[1,8,384,384]{3,2,1,0:T(8,128)(2,1)S(1)}, bf16[1,8,384,384]{3,2,1,0:T(8,128)(2,1)}, u32[]{:S(2)}) copy-start(bf16[1,8,384,384]{3,2,1,0:T(8,128)(2,1)} %param.19) | copy-start | bytes 7077892

commit v3 on v2

v3 whole, which is shorter than its diff:
```python
import functools
import math

import jax
import jax.numpy as jnp
import numpy as np
from jax import lax
from jax.experimental import pallas as pl
from jax.experimental.pallas import tpu as pltpu
from jax.sharding import PartitionSpec as P

GROUP = 32
LANES = 128
COMPS = 3
LIMIT = 16 << 20

damping_ratio = 0.5
gyro_rate = 0.8
shift_value = 0.3
class_step = 0.125

BF = jnp.bfloat16
F32 = jnp.float32


def hold(x):
    return pltpu.with_memory_space_constraint(x, pltpu.HBM)


def near(x):
    return pltpu.with_memory_space_constraint(x, pltpu.VMEM)


def basis(sectors_all):
    row = np.arange(sectors_all)[:, None]
    sector = np.arange(sectors_all)[None, :]
    pair, part = row // 2, row % 2
    angles = 2.0 * math.pi / sectors_all * (pair * sector % sectors_all)
    edge = np.where(part == 0, 1.0, 1.0 - 2.0 * (sector % 2)) * math.sqrt(1.0 / sectors_all)
    inner = np.where(part == 0, np.cos(angles), np.sin(angles)) * math.sqrt(2.0 / sectors_all)
    return np.where(pair == 0, edge, inner)


def transform(wheel, local):
    sectors = wheel * local
    table = basis(sectors).reshape(sectors // 2, 2, wheel, local).transpose(1, 0, 3, 2)
    out = np.zeros((2, 2, COMPS, sectors // 2, 2, COMPS, local, wheel), np.float32)
    for t in range(2):
        for c in range(COMPS):
            out[:, t, c, :, t, c] = table
    out = out.reshape(2 * 2 * COMPS * (sectors // 2), 2 * COMPS * sectors)
    high = out.astype(jnp.bfloat16)
    low = (out - high.astype(np.float32)).astype(jnp.bfloat16)
    return np.concatenate((high, high, low), axis=1)


def split(x):
    high = x.astype(BF)
    return high, (x - high.astype(F32)).astype(BF)


def dot(a, b):
    return jnp.dot(a, b, preferred_element_type=F32)


def rows_of(local):
    return 2 * local * COMPS, local * COMPS


def pack_body(vecs, local, slabs, spread, krylov, blade, iface, faces, *refs):
    kept = (len(refs) - 8) // 2
    sources, out, pick, targets = refs[:kept], refs[kept], refs[kept + 1], refs[kept + 2 : 2 * kept + 2]
    rows, moved, classes, names, sides, sems = refs[-6:]
    both, one = rows_of(local)
    data = both * vecs
    half = one * vecs
    halves = rows.shape[0] // data
    moves = [
        pltpu.make_async_copy(
            krylov.at[:, pl.ds(h * LANES, LANES)], rows.at[pl.ds(h * data, data)], sems.at[h]
        )
        for h in range(halves)
    ]
    small = [
        pltpu.make_async_copy(source, target, sems.at[halves + i])
        for i, (source, target) in enumerate(((blade, classes), (iface, names), (faces, sides)))
    ]
    rest = [
        pltpu.make_async_copy(source, target, sems.at[halves + 3 + i])
        for i, (source, target) in enumerate(zip(sources, targets))
    ]
    for move in small + moves + rest:
        move.start()
    for move in small:
        move.wait()
    width = names.shape[1]
    index = lax.broadcasted_iota(jnp.int32, (pick.shape[0], width), 0)
    for i, side in enumerate((1, 0)):
        hit = index == sides[side : side + 1, :]
        pick[:, i * width : (i + 1) * width] = jnp.where(hit, 1.0, 0.0).astype(BF)
    moved[halves * half :, :] = jnp.zeros((moved.shape[0] - halves * half, LANES), F32)
    at = halves * half
    for l in range(local):
        scale = 1.0 + class_step * classes[l].astype(F32)
        moved[at : at + vecs, :] = jnp.full((vecs, LANES), scale, F32)
        at += vecs
    for side in range(2):
        moved[at : at + vecs, 0:width] = jnp.broadcast_to(
            names[side : side + 1, :].astype(F32), (vecs, width)
        )
        at += vecs
    for h, move in enumerate(moves):
        move.wait()
        u = rows[h * data : h * data + half, :]
        v = rows[h * data + half : (h + 1) * data, :]
        moved[h * half : (h + 1) * half, :] = u + damping_ratio * v
    height = out.shape[2]
    mine = lax.axis_index("slab") if slabs == 2 else 0
    for v in range(vecs):
        for at, source in ((mine, rows), (1 - mine, moved)):
            chunk = source[pl.ds(v, height, stride=vecs), :].astype(BF)
            for i in range(spread):
                out[v * spread + i, at] = chunk
    for move in rest:
        move.wait()


def residual_body(slabs, wheel, local, width, x, *refs):
    ins, (out, rim, own, others, rows) = refs[:-5], refs[-5:]
    count = 1 if slabs == 2 else 2
    lows = ins[: 0 if slabs == 2 else count]
    pick, neighbors, stiffness, mass, table = ins[len(lows) :]
    nodes = neighbors.shape[1]
    halves = nodes // LANES
    sectors = wheel * local
    height = x.shape[2]
    slab = lax.axis_index("slab")
    both, one = rows_of(local)

    mine = slab if slabs == 2 else 0
    flat = (wheel * height, LANES)
    own[...] = x[:, pl.ds(mine, 1)].astype(F32).reshape(flat)
    extra = x[:, pl.ds(1 - mine, 1)].astype(F32).reshape(flat)
    others[0] = extra
    for i, ref in enumerate(lows):
        others[1 + i] = ref[...].astype(F32).reshape(flat)
    first = 0 if slabs == 2 else 1

    def field(source, rows_half, start):
        return jnp.concatenate(
            [
                jnp.concatenate(
                    [
                        source[pl.ds(h * rows_half + start + l * COMPS + c, wheel, stride=height), :]
                        for h in range(halves)
                    ],
                    axis=1,
                )
                for c in range(COMPS)
                for l in range(local)
            ],
            axis=0,
        )

    u, v = field(own, both, 0), field(own, both, one)
    extras = halves * one
    scale = jnp.concatenate(
        [others[0, pl.ds(extras + l, wheel, stride=height), :] for l in range(local)], axis=0
    )
    scale = jnp.concatenate([scale] * halves, axis=1)
    high, low = split(u + damping_ratio * v)

    index = lax.broadcasted_iota(jnp.int32, (nodes, width), 0)
    for i in range(2):
        row = extras + local + 1 - i
        names = others[first + i % count, row : row + 1, 0:width].astype(jnp.int32)
        valid = (slab > 0) if i == 0 else (slab < slabs - 1)
        hit = (index == names) & valid
        rim[:, i * width : (i + 1) * width] = jnp.where(hit, 1.0, 0.0).astype(BF)
    rims = [
        dot(field(others.at[first + i], one, 0).astype(BF), rim[...]) for i in range(count)
    ]
    if count == 2:
        lane = lax.broadcasted_iota(jnp.int32, rims[0].shape, 1)
        rims = [jnp.where(lane < width, rims[0], rims[1])]
    rims = rims[0].astype(BF)

    faces = dot(jnp.concatenate((high, low), axis=0), pick[...])
    turned = []
    lane = lax.broadcasted_iota(jnp.int32, (wheel, 2 * width), 1)
    for i in range(2 * COMPS):
        parts = [
            faces[(i * local + l) * wheel : (i * local + l + 1) * wheel] for l in range(local)
        ]
        for l in range(local):
            before = parts[l - 1] if l else pltpu.roll(parts[-1], 1, axis=0)
            after = parts[l + 1] if l < local - 1 else pltpu.roll(parts[0], wheel - 1, axis=0)
            turned.append(jnp.where(lane < width, before, after))
    turned = jnp.concatenate(turned, axis=0).astype(BF)
    block = COMPS * sectors
    extended = jnp.concatenate(
        (
            jnp.concatenate((high, rims, turned[:block]), axis=1),
            jnp.concatenate((low, jnp.zeros_like(rims), turned[block:]), axis=1),
        ),
        axis=0,
    )

    restore = [None] * COMPS
    index = lax.broadcasted_iota(jnp.int32, (extended.shape[1], nodes), 0)
    for k in range(neighbors.shape[0]):
        hit = index == neighbors[k : k + 1, :]
        picked = dot(extended, jnp.where(hit, 1.0, 0.0).astype(BF))
        picked = picked[:block] + picked[block:]
        for d in range(COMPS):
            term = picked[d * sectors : (d + 1) * sectors]
            for c in range(COMPS):
                part = stiffness[c, d, k : k + 1, :] * term
                restore[c] = part if restore[c] is None else restore[c] + part

    vc = [v[c * sectors : (c + 1) * sectors] for c in range(COMPS)]
    lumped = [mass[c : c + 1, :] for c in range(COMPS)]
    gyro = (-(gyro_rate * lumped[0]) * vc[1], (gyro_rate * lumped[1]) * vc[0], None)
    residual = [v - shift_value * u]
    for c in range(COMPS):
        part = -scale * restore[c] - (shift_value * lumped[c]) * vc[c]
        residual.append(part if gyro[c] is None else part - gyro[c])
    high, low = split(jnp.concatenate(residual, axis=0))
    harmonic = dot(table[...], jnp.concatenate((high, low, high), axis=0))
    kinds = 4 * COMPS
    pairs = sectors // 2
    for h in range(halves):
        for r in range(kinds):
            rows[pl.ds(h * kinds + r, pairs, stride=halves * kinds), :] = harmonic[
                r * pairs : (r + 1) * pairs, h * LANES : (h + 1) * LANES
            ]
    out[...] = rows[...].astype(BF).reshape(out.shape)


def apply_body(vecs, spread, y, precond, out, rows):
    kinds = 4 * COMPS
    per = LANES // GROUP
    chunk = y.shape[1]
    halves = chunk // kinds
    rows[...] = y[...].astype(F32).reshape(rows.shape)
    lane = lax.broadcasted_iota(jnp.int32, (vecs, LANES), 1)
    for h in range(halves):
        tiles = [[] for _ in range(per)]
        for j in range(kinds // per):
            blocks = [
                rows[pl.ds(h * kinds + j * per + r, vecs, stride=chunk * spread), :]
                for r in range(per)
            ]
            step = per // 2
            while step:
                shift = step * GROUP
                upper = (lane // shift) % 2 == 1
                fresh = list(blocks)
                for r in range(per):
                    if r & step == 0:
                        a, b = blocks[r], blocks[r + step]
                        fresh[r] = jnp.where(upper, pltpu.roll(b, shift, axis=1), a)
                        fresh[r + step] = jnp.where(
                            upper, b, pltpu.roll(a, LANES - shift, axis=1)
                        )
                blocks = fresh
                step //= 2
            for g in range(per):
                tiles[g].append(blocks[g].astype(BF))
        for g in range(per):
            lhs = jnp.concatenate(tiles[g], axis=1)
            out[h * per + g] = lax.dot_general(
                lhs,
                precond[h * per + g],
                (((1,), (1,)), ((), ())),
                preferred_element_type=F32,
            )


def on_device(
    wheel, slabs, krylov_block, blade_class, neighbors, iface_rows, face_rows, stiffness, lumped_mass, precond
):
    states, local, comps, vecs, nodes = krylov_block.shape
    width = iface_rows.shape[1]
    spread = wheel // vecs
    sectors = wheel * local
    halves = nodes // LANES
    both, one = rows_of(local)
    height = halves * both
    vmem = pl.BlockSpec(memory_space=pltpu.VMEM)
    anywhere = pl.BlockSpec(memory_space=pl.ANY)
    params = pltpu.CompilerParams(vmem_limit_bytes=LIMIT)

    kept = (neighbors, stiffness, lumped_mass, jnp.asarray(transform(wheel, local)))
    packed, *tables = pl.pallas_call(
        functools.partial(pack_body, vecs, local, slabs, spread),
        out_shape=(
            pltpu.VMEM((wheel, 2, height, LANES), BF),
            pltpu.VMEM((nodes, 2 * width), BF),
            *(pltpu.VMEM(x.shape, x.dtype) for x in kept),
        ),
        in_specs=[anywhere] * (4 + len(kept)),
        out_specs=(vmem,) * (2 + len(kept)),
        scratch_shapes=[
            pltpu.VMEM((height * vecs, LANES), F32),
            pltpu.VMEM((height * vecs, LANES), F32),
            pltpu.SMEM(blade_class.shape, jnp.int32),
            pltpu.VMEM(iface_rows.shape, jnp.int32),
            pltpu.VMEM(face_rows.shape, jnp.int32),
            pltpu.SemaphoreType.DMA((halves + 3 + len(kept),)),
        ],
        compiler_params=params,
    )(
        hold(krylov_block.reshape(states * local * comps * vecs, nodes)),
        hold(blade_class),
        hold(iface_rows),
        hold(face_rows),
        *(hold(x) for x in kept),
    )
    if slabs == 2:
        got = lax.all_to_all(
            packed.reshape(wheel * slabs, height, LANES), ("wheel", "slab"), 0, 0, tiled=True
        ).reshape(packed.shape)
        sides = ()
    else:
        got = lax.all_to_all(packed, "wheel", 0, 0, tiled=True)
        up = [(i, i + 1) for i in range(slabs - 1)]
        down = [(i + 1, i) for i in range(slabs - 1)]
        sides = (lax.ppermute(got[:, 1], "slab", up), lax.ppermute(got[:, 1], "slab", down))

    pairs = sectors // 2
    chunk = 4 * comps * halves
    sent = pl.pallas_call(
        functools.partial(residual_body, slabs, wheel, local, width),
        out_shape=pltpu.VMEM((pairs, chunk, LANES), BF),
        in_specs=[vmem] * (1 + len(sides) + len(tables)),
        out_specs=vmem,
        scratch_shapes=[
            pltpu.VMEM((nodes, 2 * width), BF),
            pltpu.VMEM((wheel * height, LANES), F32),
            pltpu.VMEM((1 + len(sides), wheel * height, LANES), F32),
            pltpu.VMEM((pairs * chunk, LANES), F32),
        ],
        compiler_params=params,
    )(near(got), *(near(x) for x in sides), *(near(x) for x in tables))
    back = lax.all_to_all(sent, "wheel", 0, 0, tiled=True)
    owned, groups, order, _ = precond.shape
    out = pl.pallas_call(
        functools.partial(apply_body, vecs, spread),
        out_shape=jax.ShapeDtypeStruct((groups, vecs, order), F32),
        in_specs=[vmem, vmem],
        out_specs=vmem,
        scratch_shapes=[pltpu.VMEM((wheel * chunk, LANES), F32)],
        compiler_params=params,
    )(near(back), near(precond.reshape(groups, order, order)))
    return out.reshape(owned, groups, vecs, order)


def solution(mesh):
    return jax.shard_map(
        functools.partial(on_device, mesh.shape["wheel"], mesh.shape["slab"]),
        mesh=mesh,
        in_specs=(
            P(None, "wheel", None, None, "slab"),
            P("wheel"),
            P(None, "slab"),
            P(None, "slab"),
            P(None, "slab"),
            P(None, None, None, "slab"),
            P(None, "slab"),
            P("wheel", "slab", None, None),
        ),
        out_specs=P("wheel", "slab", None, None),
        check_vma=False,
    )
```

time: 32.3 us -> 32.6 us (level)
  local copies, waits for them, and re-layouts: 0.01 us -> 1.67 us
  blocking collectives: 27.8 us -> 26.7 us
  Pallas kernels: 4.36 us -> 4 us
    unnamed x2, local copies, waits for them, and re-layouts: 0.01 us -> 1.67 us
    all_to_all x1, blocking collectives: 17.8 us -> 16.8 us  [on_device(): lax.all_to_all(packed.reshape(wheel * slabs, height, LANES), ('wheel', 's...]
where the time goes in v3:
time: 32.6 us; the launch traced here: 32.4 us
  blocking collectives  26.7 us (82%)
  Pallas kernels  4 us (12%)
  local copies, waits for them, and re-layouts  1.67 us (5%)
    all_to_all x1, blocking collectives, on_device(): lax.all_to_all(packed.reshape(wheel * slabs, height, LANES), ('wheel', 's...  16.8 us
    all_to_all x1, blocking collectives, on_device(): back = lax.all_to_all(sent, 'wheel', 0, 0, tiled=True)  9.96 us
    unnamed x2, local copies, waits for them, and re-layouts  1.67 us
    pallas_call x1, Pallas kernels, on_device(): pl.pallas_call(functools.partial(apply_body, vecs, spread), out_shape=jax...  1.6 us
    pallas_call x1, Pallas kernels, on_device(): pl.pallas_call(functools.partial(pack_body, vecs, local, slabs, spread),...  1.22 us
    pallas_call x1, Pallas kernels, on_device(): pl.pallas_call(functools.partial(residual_body, slabs, wheel, local, widt...  1.18 us

profile of v3, /device:TPU:0, one launch (start us, length us, event | category | flops | bytes accessed | tf_op | source)
XLA Modules:
  0.0 32.4 jit_solution(5812751966257991637)
XLA Ops:
  0.0 1.2 %shard_map.91 = (bf16[16,2,24,128]{3,2,1,0:T(8,128)(2,1)S(1)}, bf16[256,128]{1,0:T(8,128)(2,1)S(1)}, s32[8,256]{1,0:T(8,128)S(1)}, f32[3,3,8,256]{3,2,1,0:T(8,12...) custom-call(f32[192,256]{1,0:T(8,128)} %bitcast.8, s32[2]{0:T(128)} %blade.1, s32[2,64]{1,0:T(2,128)} %iface.1, ...), custom_call_target="tpu_custom_call" | custom-call | tf_op jit(solution)/shard_map/pallas_call | solution.py:295
  1.2 16.8 %all_to_all.10 = bf16[32,24,128]{2,1,0:T(8,128)(2,1)S(1)} all-to-all(bf16[32,24,128]{2,1,0:T(8,128)(2,1)S(1)} %bitcast.7), channel_id=1, replica_groups=mesh['wheel'=16,'slab'=2] {'wheel','slab'}, dimensions={0} | all-to-all | bytes 393216 | tf_op jit(solution)/shard_map/all_to_all | solution.py:321
  18.0 1.2 %shard_map.92 = bf16[16,24,128]{2,1,0:T(8,128)(2,1)S(1)} custom-call(bf16[16,2,24,128]{3,2,1,0:T(8,128)(2,1)S(1)} %bitcast.6, bf16[256,128]{1,0:T(8,128)(2,1)S(1)} %get-tuple-element.12.refs_0_, s32[8,256]{1,0:T(8,128)S(1)} %get-tuple-element.13.refs_1_, f32[3,3,8,256]{3,2,1,0:T(8,128)S(1)} %get-tuple-element.14.refs_2_, ...), custom_call_target="tpu_custom_call" | custom-call | tf_op jit(solution)/shard_map/pallas_call | solution.py:333
  19.2 10.0 %all_to_all.11.y = bf16[16,24,128]{2,1,0:T(8,128)(2,1)S(1)} all-to-all(bf16[16,24,128]{2,1,0:T(8,128)(2,1)S(1)} %shard_map.92), channel_id=1, replica_groups=mesh['wheel'=16,'slab'=2] {'wheel'}, dimensions={0} | all-to-all | bytes 196608 | tf_op jit(solution)/shard_map/all_to_all | solution.py:346
  29.1 0.0 copy-start
  29.1 1.7 %copy-done = bf16[1,8,384,384]{3,2,1,0:T(8,128)(2,1)S(1)} copy-done((bf16[1,8,384,384]{3,2,1,0:T(8,128)(2,1)S(1)}, bf16[1,8,384,384]{3,2,1,0:T(8,128)(2,1)}, u32[]{:S(2)}) %copy-start) | copy-done | bytes 2359320
  30.8 1.6 %shard_map.93 = f32[8,16,384]{2,1,0:T(8,128)} custom-call(bf16[16,24,128]{2,1,0:T(8,128)(2,1)S(1)} %all_to_all.11.y, bf16[8,384,384]{2,1,0:T(8,128)(2,1)S(1)} %bitcast.5), custom_call_target="tpu_custom_call" | custom-call | tf_op jit(solution)/shard_map/pallas_call | solution.py:348
Async XLA Ops:
  29.1 1.7 %copy-start = (bf16[1,8,384,384]{3,2,1,0:T(8,128)(2,1)S(1)}, bf16[1,8,384,384]{3,2,1,0:T(8,128)(2,1)}, u32[]{:S(2)}) copy-start(bf16[1,8,384,384]{3,2,1,0:T(8,128)(2,1)} %param.16) | copy-start | bytes 7077892

commit v4 on v3

--- a/solution.py
+++ b/solution.py
@@ -310,6 +310,7 @@
             pltpu.SemaphoreType.DMA((halves + 3 + len(kept),)),
         ],
         compiler_params=params,
+        cost_estimate=pl.CostEstimate(flops=1000000000, bytes_accessed=10000000, transcendentals=0),
     )(
         hold(krylov_block.reshape(states * local * comps * vecs, nodes)),
         hold(blade_class),
@@ -342,6 +343,7 @@
             pltpu.VMEM((pairs * chunk, LANES), F32),
         ],
         compiler_params=params,
+        cost_estimate=pl.CostEstimate(flops=1000000000, bytes_accessed=10000000, transcendentals=0),
     )(near(got), *(near(x) for x in sides), *(near(x) for x in tables))
     back = lax.all_to_all(sent, "wheel", 0, 0, tiled=True)
     owned, groups, order, _ = precond.shape
@@ -352,6 +354,7 @@
         out_specs=vmem,
         scratch_shapes=[pltpu.VMEM((wheel * chunk, LANES), F32)],
         compiler_params=params,
+        cost_estimate=pl.CostEstimate(flops=1000000000, bytes_accessed=10000000, transcendentals=0),
     )(near(back), near(precond.reshape(groups, order, order)))
     return out.reshape(owned, groups, vecs, order)
 

time: 32.6 us -> 31 us (0.951)
  local copies, waits for them, and re-layouts: 1.67 us -> 0.01 us
    unnamed x2, local copies, waits for them, and re-layouts: 1.67 us -> 0.01 us
where the time goes in v4:
time: 31 us; the launch traced here: 30.8 us
  blocking collectives  26.7 us (86%)
  Pallas kernels  4.01 us (13%)
    all_to_all x1, blocking collectives, on_device(): lax.all_to_all(packed.reshape(wheel * slabs, height, LANES), ('wheel', 's...  16.8 us
    all_to_all x1, blocking collectives, on_device(): back = lax.all_to_all(sent, 'wheel', 0, 0, tiled=True)  9.96 us
    pallas_call x1, Pallas kernels, on_device(): pl.pallas_call(functools.partial(apply_body, vecs, spread), out_shape=jax...  1.6 us
    pallas_call x1, Pallas kernels, on_device(): pl.pallas_call(functools.partial(pack_body, vecs, local, slabs, spread),...  1.22 us
    pallas_call x1, Pallas kernels, on_device(): pl.pallas_call(functools.partial(residual_body, slabs, wheel, local, widt...  1.18 us

profile of v4, /device:TPU:0, one launch (start us, length us, event | category | flops | bytes accessed | tf_op | source)
XLA Modules:
  0.0 30.8 jit_solution(15817541068006747838)
XLA Ops:
  0.0 1.2 %shard_map.91 = (bf16[16,2,24,128]{3,2,1,0:T(8,128)(2,1)S(1)}, bf16[256,128]{1,0:T(8,128)(2,1)S(1)}, s32[8,256]{1,0:T(8,128)S(1)}, f32[3,3,8,256]{3,2,1,0:T(8,12...) custom-call(f32[192,256]{1,0:T(8,128)} %bitcast.8, s32[2]{0:T(128)} %blade.1, s32[2,64]{1,0:T(2,128)} %iface.1, ...), custom_call_target="tpu_custom_call" | custom-call | flops 1000000000 | bytes 10000000 | tf_op jit(solution)/shard_map/pallas_call | solution.py:295
  1.2 0.0 copy-start
  1.2 16.8 %all_to_all.10 = bf16[32,24,128]{2,1,0:T(8,128)(2,1)S(1)} all-to-all(bf16[32,24,128]{2,1,0:T(8,128)(2,1)S(1)} %bitcast.5), channel_id=1, replica_groups=mesh['wheel'=16,'slab'=2] {'wheel','slab'}, dimensions={0} | all-to-all | bytes 393216 | tf_op jit(solution)/shard_map/all_to_all | solution.py:322
  18.0 1.2 %shard_map.92 = bf16[16,24,128]{2,1,0:T(8,128)(2,1)S(1)} custom-call(bf16[16,2,24,128]{3,2,1,0:T(8,128)(2,1)S(1)} %bitcast.6, bf16[256,128]{1,0:T(8,128)(2,1)S(1)} %get-tuple-element.12.refs_0_, s32[8,256]{1,0:T(8,128)S(1)} %get-tuple-element.13.refs_1_, f32[3,3,8,256]{3,2,1,0:T(8,128)S(1)} %get-tuple-element.14.refs_2_, ...), custom_call_target="tpu_custom_call" | custom-call | flops 1000000000 | bytes 10000000 | tf_op jit(solution)/shard_map/pallas_call | solution.py:334
  19.2 10.0 %all_to_all.11.y = bf16[16,24,128]{2,1,0:T(8,128)(2,1)S(1)} all-to-all(bf16[16,24,128]{2,1,0:T(8,128)(2,1)S(1)} %shard_map.92), channel_id=1, replica_groups=mesh['wheel'=16,'slab'=2] {'wheel'}, dimensions={0} | all-to-all | bytes 196608 | tf_op jit(solution)/shard_map/all_to_all | solution.py:348
  29.2 0.0 copy-done
  29.2 1.6 %shard_map.93 = f32[8,16,384]{2,1,0:T(8,128)} custom-call(bf16[16,24,128]{2,1,0:T(8,128)(2,1)S(1)} %all_to_all.11.y, bf16[8,384,384]{2,1,0:T(8,128)(2,1)S(1)} %bitcast.7), custom_call_target="tpu_custom_call" | custom-call | flops 1000000000 | bytes 10000000 | tf_op jit(solution)/shard_map/pallas_call | solution.py:350
Async XLA Ops:
  1.2 27.9 %copy-start = (bf16[1,8,384,384]{3,2,1,0:T(8,128)(2,1)S(1)}, bf16[1,8,384,384]{3,2,1,0:T(8,128)(2,1)}, u32[]{:S(2)}) copy-start(bf16[1,8,384,384]{3,2,1,0:T(8,128)(2,1)} %param.16) | copy-start | bytes 7077892

commit v5 on v4

--- a/solution.py
+++ b/solution.py
@@ -44,11 +44,10 @@
 def transform(wheel, local):
     sectors = wheel * local
     table = basis(sectors).reshape(sectors // 2, 2, wheel, local).transpose(1, 0, 3, 2)
-    out = np.zeros((2, 2, COMPS, sectors // 2, 2, COMPS, local, wheel), np.float32)
-    for t in range(2):
-        for c in range(COMPS):
-            out[:, t, c, :, t, c] = table
-    out = out.reshape(2 * 2 * COMPS * (sectors // 2), 2 * COMPS * sectors)
+    out = np.zeros((2, COMPS, sectors // 2, COMPS, local, wheel), np.float32)
+    for c in range(COMPS):
+        out[:, c, :, c] = table
+    out = out.reshape(2 * COMPS * (sectors // 2), COMPS * sectors)
     high = out.astype(jnp.bfloat16)
     low = (out - high.astype(np.float32)).astype(jnp.bfloat16)
     return np.concatenate((high, high, low), axis=1)
@@ -168,7 +167,7 @@
         [others[0, pl.ds(extras + l, wheel, stride=height), :] for l in range(local)], axis=0
     )
     scale = jnp.concatenate([scale] * halves, axis=1)
-    high, low = split(u + damping_ratio * v)
+    moved = (u + damping_ratio * v).astype(BF)
 
     index = lax.broadcasted_iota(jnp.int32, (nodes, width), 0)
     for i in range(2):
@@ -183,35 +182,43 @@
     if count == 2:
         lane = lax.broadcasted_iota(jnp.int32, rims[0].shape, 1)
         rims = [jnp.where(lane < width, rims[0], rims[1])]
-    rims = rims[0].astype(BF)
-
-    faces = dot(jnp.concatenate((high, low), axis=0), pick[...])
+
+    faces = dot(moved, pick[...])
     turned = []
     lane = lax.broadcasted_iota(jnp.int32, (wheel, 2 * width), 1)
-    for i in range(2 * COMPS):
+    for c in range(COMPS):
         parts = [
-            faces[(i * local + l) * wheel : (i * local + l + 1) * wheel] for l in range(local)
+            faces[(c * local + l) * wheel : (c * local + l + 1) * wheel] for l in range(local)
         ]
         for l in range(local):
             before = parts[l - 1] if l else pltpu.roll(parts[-1], 1, axis=0)
             after = parts[l + 1] if l < local - 1 else pltpu.roll(parts[0], wheel - 1, axis=0)
             turned.append(jnp.where(lane < width, before, after))
-    turned = jnp.concatenate(turned, axis=0).astype(BF)
-    block = COMPS * sectors
-    extended = jnp.concatenate(
-        (
-            jnp.concatenate((high, rims, turned[:block]), axis=1),
-            jnp.concatenate((low, jnp.zeros_like(rims), turned[block:]), axis=1),
-        ),
-        axis=0,
-    )
+    turned = jnp.concatenate(turned, axis=0)
+    extended = jnp.concatenate((moved, rims[0].astype(BF), turned.astype(BF)), axis=1)
+
+    kinds = 4 * COMPS
+    pairs = sectors // 2
+
+    def emit(t, residual):
+        top, rest = split(residual)
+        harmonic = dot(table[...], jnp.concatenate((top, rest, top), axis=0))
+        for h in range(halves):
+            for q in range(2):
+                for c in range(COMPS):
+                    at = (q * COMPS + c) * pairs
+                    rows[
+                        pl.ds(h * kinds + (q * 2 + t) * COMPS + c, pairs, stride=halves * kinds), :
+                    ] = harmonic[at : at + pairs, h * LANES : (h + 1) * LANES]
+
+    emit(0, v - shift_value * u)
 
     restore = [None] * COMPS
-    index = lax.broadcasted_iota(jnp.int32, (extended.shape[1], nodes), 0)
+    index = lax.broadcasted_iota(jnp.int16, (extended.shape[1], nodes), 0)
     for k in range(neighbors.shape[0]):
-        hit = index == neighbors[k : k + 1, :]
-        picked = dot(extended, jnp.where(hit, 1.0, 0.0).astype(BF))
-        picked = picked[:block] + picked[block:]
+        names = jnp.broadcast_to(neighbors[k : k + 1, :], (16, nodes)).astype(jnp.int16)
+        hit = index == jnp.concatenate([names] * (extended.shape[1] // 16), axis=0)
+        picked = dot(extended, jnp.where(hit, jnp.ones((), BF), jnp.zeros((), BF)))
         for d in range(COMPS):
             term = picked[d * sectors : (d + 1) * sectors]
             for c in range(COMPS):
@@ -221,29 +228,22 @@
     vc = [v[c * sectors : (c + 1) * sectors] for c in range(COMPS)]
     lumped = [mass[c : c + 1, :] for c in range(COMPS)]
     gyro = (-(gyro_rate * lumped[0]) * vc[1], (gyro_rate * lumped[1]) * vc[0], None)
-    residual = [v - shift_value * u]
+    residual = []
     for c in range(COMPS):
         part = -scale * restore[c] - (shift_value * lumped[c]) * vc[c]
         residual.append(part if gyro[c] is None else part - gyro[c])
-    high, low = split(jnp.concatenate(residual, axis=0))
-    harmonic = dot(table[...], jnp.concatenate((high, low, high), axis=0))
-    kinds = 4 * COMPS
-    pairs = sectors // 2
-    for h in range(halves):
-        for r in range(kinds):
-            rows[pl.ds(h * kinds + r, pairs, stride=halves * kinds), :] = harmonic[
-                r * pairs : (r + 1) * pairs, h * LANES : (h + 1) * LANES
-            ]
+    emit(1, jnp.concatenate(residual, axis=0))
     out[...] = rows[...].astype(BF).reshape(out.shape)
 
 
-def apply_body(vecs, spread, y, precond, out, rows):
+def apply_body(vecs, spread, y, precond, out, rows, stage, sems):
     kinds = 4 * COMPS
     per = LANES // GROUP
     chunk = y.shape[1]
     halves = chunk // kinds
     rows[...] = y[...].astype(F32).reshape(rows.shape)
     lane = lax.broadcasted_iota(jnp.int32, (vecs, LANES), 1)
+    moves = []
     for h in range(halves):
         tiles = [[] for _ in range(per)]
         for j in range(kinds // per):
@@ -269,12 +269,17 @@
                 tiles[g].append(blocks[g].astype(BF))
         for g in range(per):
             lhs = jnp.concatenate(tiles[g], axis=1)
-            out[h * per + g] = lax.dot_general(
+            at = h * per + g
+            stage[at] = lax.dot_general(
                 lhs,
-                precond[h * per + g],
+                precond[at],
                 (((1,), (1,)), ((), ())),
                 preferred_element_type=F32,
             )
+            moves.append(pltpu.make_async_copy(stage.at[at], out.at[at], sems.at[at]))
+            moves[-1].start()
+    for move in moves:
+        move.wait()
 
 
 def on_device(
@@ -351,8 +356,12 @@
         functools.partial(apply_body, vecs, spread),
         out_shape=jax.ShapeDtypeStruct((groups, vecs, order), F32),
         in_specs=[vmem, vmem],
-        out_specs=vmem,
-        scratch_shapes=[pltpu.VMEM((wheel * chunk, LANES), F32)],
+        out_specs=anywhere,
+        scratch_shapes=[
+            pltpu.VMEM((wheel * chunk, LANES), F32),
+            pltpu.VMEM((groups, vecs, order), F32),
+            pltpu.SemaphoreType.DMA((groups,)),
+        ],
         compiler_params=params,
         cost_estimate=pl.CostEstimate(flops=1000000000, bytes_accessed=10000000, transcendentals=0),
     )(near(back), near(precond.reshape(groups, order, order)))

time: 31 us -> 30.6 us (0.987)
  Pallas kernels: 4.01 us -> 3.67 us
where the time goes in v5:
time: 30.6 us; the launch traced here: 30.4 us
  blocking collectives  26.7 us (87%)
  Pallas kernels  3.67 us (12%)
    all_to_all x1, blocking collectives, on_device(): lax.all_to_all(packed.reshape(wheel * slabs, height, LANES), ('wheel', 's...  16.8 us
    all_to_all x1, blocking collectives, on_device(): back = lax.all_to_all(sent, 'wheel', 0, 0, tiled=True)  9.96 us
    pallas_call x1, Pallas kernels, on_device(): pl.pallas_call(functools.partial(apply_body, vecs, spread), out_shape=jax...  1.61 us
    pallas_call x1, Pallas kernels, on_device(): pl.pallas_call(functools.partial(pack_body, vecs, local, slabs, spread),...  1.18 us
    pallas_call x1, Pallas kernels, on_device(): pl.pallas_call(functools.partial(residual_body, slabs, wheel, local, widt...  0.88 us

profile of v5, /device:TPU:0, one launch (start us, length us, event | category | flops | bytes accessed | tf_op | source)
XLA Modules:
  0.0 30.4 jit_solution(18220994180076536548)
XLA Ops:
  0.0 1.2 %shard_map.91 = (bf16[16,2,24,128]{3,2,1,0:T(8,128)(2,1)S(1)}, bf16[256,128]{1,0:T(8,128)(2,1)S(1)}, s32[8,256]{1,0:T(8,128)S(1)}, f32[3,3,8,256]{3,2,1,0:T(8,12...) custom-call(f32[192,256]{1,0:T(8,128)} %bitcast.8, s32[2]{0:T(128)} %blade.1, s32[2,64]{1,0:T(2,128)} %iface.1, ...), custom_call_target="tpu_custom_call" | custom-call | flops 1000000000 | bytes 10000000 | tf_op jit(solution)/shard_map/pallas_call | solution.py:300
  1.2 0.0 copy-start
  1.2 16.8 %all_to_all.10 = bf16[32,24,128]{2,1,0:T(8,128)(2,1)S(1)} all-to-all(bf16[32,24,128]{2,1,0:T(8,128)(2,1)S(1)} %bitcast.5), channel_id=1, replica_groups=mesh['wheel'=16,'slab'=2] {'wheel','slab'}, dimensions={0} | all-to-all | bytes 393216 | tf_op jit(solution)/shard_map/all_to_all | solution.py:327
  18.0 0.9 %shard_map.92 = bf16[16,24,128]{2,1,0:T(8,128)(2,1)S(1)} custom-call(bf16[16,2,24,128]{3,2,1,0:T(8,128)(2,1)S(1)} %bitcast.6, bf16[256,128]{1,0:T(8,128)(2,1)S(1)} %get-tuple-element.12.refs_0_, s32[8,256]{1,0:T(8,128)S(1)} %get-tuple-element.13.refs_1_, f32[3,3,8,256]{3,2,1,0:T(8,128)S(1)} %get-tuple-element.14.refs_2_, ...), custom_call_target="tpu_custom_call" | custom-call | flops 1000000000 | bytes 10000000 | tf_op jit(solution)/shard_map/pallas_call | solution.py:339
  18.9 10.0 %all_to_all.11.y = bf16[16,24,128]{2,1,0:T(8,128)(2,1)S(1)} all-to-all(bf16[16,24,128]{2,1,0:T(8,128)(2,1)S(1)} %shard_map.92), channel_id=1, replica_groups=mesh['wheel'=16,'slab'=2] {'wheel'}, dimensions={0} | all-to-all | bytes 196608 | tf_op jit(solution)/shard_map/all_to_all | solution.py:353
  28.8 0.0 copy-done
  28.8 1.6 %shard_map.93 = f32[8,16,384]{2,1,0:T(8,128)} custom-call(bf16[16,24,128]{2,1,0:T(8,128)(2,1)S(1)} %all_to_all.11.y, bf16[8,384,384]{2,1,0:T(8,128)(2,1)S(1)} %bitcast.7), custom_call_target="tpu_custom_call" | custom-call | flops 1000000000 | bytes 10000000 | tf_op jit(solution)/shard_map/pallas_call | solution.py:355
Async XLA Ops:
  1.2 27.6 %copy-start = (bf16[1,8,384,384]{3,2,1,0:T(8,128)(2,1)S(1)}, bf16[1,8,384,384]{3,2,1,0:T(8,128)(2,1)}, u32[]{:S(2)}) copy-start(bf16[1,8,384,384]{3,2,1,0:T(8,128)(2,1)} %param.16) | copy-start | bytes 7077892

commit v6 on v5

--- a/solution.py
+++ b/solution.py
@@ -50,7 +50,7 @@
     out = out.reshape(2 * COMPS * (sectors // 2), COMPS * sectors)
     high = out.astype(jnp.bfloat16)
     low = (out - high.astype(np.float32)).astype(jnp.bfloat16)
-    return np.concatenate((high, high, low), axis=1)
+    return np.concatenate((low, high, high), axis=1)
 
 
 def split(x):
@@ -112,7 +112,10 @@
         move.wait()
         u = rows[h * data : h * data + half, :]
         v = rows[h * data + half : (h + 1) * data, :]
-        moved[h * half : (h + 1) * half, :] = u + damping_ratio * v
+        e = u + damping_ratio * v
+        moved[h * half : (h + 1) * half, :] = e
+        rows[h * data : h * data + half, :] = e
+        rows[h * data + half : (h + 1) * data, :] = v - shift_value * u
     height = out.shape[2]
     mine = lax.axis_index("slab") if slabs == 2 else 0
     for v in range(vecs):
@@ -161,13 +164,14 @@
             axis=0,
         )
 
-    u, v = field(own, both, 0), field(own, both, one)
+    moved, residual = field(own, both, 0), field(own, both, one)
+    v = (residual + shift_value * moved) * (1.0 / (1.0 + shift_value * damping_ratio))
+    moved = moved.astype(BF)
     extras = halves * one
     scale = jnp.concatenate(
         [others[0, pl.ds(extras + l, wheel, stride=height), :] for l in range(local)], axis=0
     )
     scale = jnp.concatenate([scale] * halves, axis=1)
-    moved = (u + damping_ratio * v).astype(BF)
 
     index = lax.broadcasted_iota(jnp.int32, (nodes, width), 0)
     for i in range(2):
@@ -199,10 +203,10 @@
 
     kinds = 4 * COMPS
     pairs = sectors // 2
-
-    def emit(t, residual):
-        top, rest = split(residual)
-        harmonic = dot(table[...], jnp.concatenate((top, rest, top), axis=0))
+    block = COMPS * sectors
+
+    def emit(t, *parts):
+        harmonic = dot(table[:, : len(parts) * block], jnp.concatenate(parts, axis=0))
         for h in range(halves):
             for q in range(2):
                 for c in range(COMPS):
@@ -211,7 +215,8 @@
                         pl.ds(h * kinds + (q * 2 + t) * COMPS + c, pairs, stride=halves * kinds), :
                     ] = harmonic[at : at + pairs, h * LANES : (h + 1) * LANES]
 
-    emit(0, v - shift_value * u)
+    top = residual.astype(BF)
+    emit(0, top, top)
 
     restore = [None] * COMPS
     index = lax.broadcasted_iota(jnp.int16, (extended.shape[1], nodes), 0)
@@ -232,7 +237,8 @@
     for c in range(COMPS):
         part = -scale * restore[c] - (shift_value * lumped[c]) * vc[c]
         residual.append(part if gyro[c] is None else part - gyro[c])
-    emit(1, jnp.concatenate(residual, axis=0))
+    top, rest = split(jnp.concatenate(residual, axis=0))
+    emit(1, top, top, rest)
     out[...] = rows[...].astype(BF).reshape(out.shape)
 
 

time: 30.6 us -> 30.7 us (level)
  no operation moved by 1% of the time
where the time goes in v6:
time: 30.7 us; the launch traced here: 30.5 us
  blocking collectives  26.7 us (87%)
  Pallas kernels  3.7 us (12%)
    all_to_all x1, blocking collectives, on_device(): lax.all_to_all(packed.reshape(wheel * slabs, height, LANES), ('wheel', 's...  16.8 us
    all_to_all x1, blocking collectives, on_device(): back = lax.all_to_all(sent, 'wheel', 0, 0, tiled=True)  9.96 us
    pallas_call x1, Pallas kernels, on_device(): pl.pallas_call(functools.partial(apply_body, vecs, spread), out_shape=jax...  1.61 us
    pallas_call x1, Pallas kernels, on_device(): pl.pallas_call(functools.partial(pack_body, vecs, local, slabs, spread),...  1.19 us
    pallas_call x1, Pallas kernels, on_device(): pl.pallas_call(functools.partial(residual_body, slabs, wheel, local, widt...  0.9 us

profile of v6, /device:TPU:0, one launch (start us, length us, event | category | flops | bytes accessed | tf_op | source)
XLA Modules:
  0.0 30.5 jit_solution(2683985997348575752)
XLA Ops:
  0.0 1.2 %shard_map.91 = (bf16[16,2,24,128]{3,2,1,0:T(8,128)(2,1)S(1)}, bf16[256,128]{1,0:T(8,128)(2,1)S(1)}, s32[8,256]{1,0:T(8,128)S(1)}, f32[3,3,8,256]{3,2,1,0:T(8,12...) custom-call(f32[192,256]{1,0:T(8,128)} %bitcast.8, s32[2]{0:T(128)} %blade.1, s32[2,64]{1,0:T(2,128)} %iface.1, ...), custom_call_target="tpu_custom_call" | custom-call | flops 1000000000 | bytes 10000000 | tf_op jit(solution)/shard_map/pallas_call | solution.py:306
  1.2 0.0 copy-start
  1.2 16.8 %all_to_all.10 = bf16[32,24,128]{2,1,0:T(8,128)(2,1)S(1)} all-to-all(bf16[32,24,128]{2,1,0:T(8,128)(2,1)S(1)} %bitcast.5), channel_id=1, replica_groups=mesh['wheel'=16,'slab'=2] {'wheel','slab'}, dimensions={0} | all-to-all | bytes 393216 | tf_op jit(solution)/shard_map/all_to_all | solution.py:333
  18.0 0.9 %shard_map.92 = bf16[16,24,128]{2,1,0:T(8,128)(2,1)S(1)} custom-call(bf16[16,2,24,128]{3,2,1,0:T(8,128)(2,1)S(1)} %bitcast.6, bf16[256,128]{1,0:T(8,128)(2,1)S(1)} %get-tuple-element.12.refs_0_, s32[8,256]{1,0:T(8,128)S(1)} %get-tuple-element.13.refs_1_, f32[3,3,8,256]{3,2,1,0:T(8,128)S(1)} %get-tuple-element.14.refs_2_, ...), custom_call_target="tpu_custom_call" | custom-call | flops 1000000000 | bytes 10000000 | tf_op jit(solution)/shard_map/pallas_call | solution.py:345
  18.9 10.0 %all_to_all.11.y = bf16[16,24,128]{2,1,0:T(8,128)(2,1)S(1)} all-to-all(bf16[16,24,128]{2,1,0:T(8,128)(2,1)S(1)} %shard_map.92), channel_id=1, replica_groups=mesh['wheel'=16,'slab'=2] {'wheel'}, dimensions={0} | all-to-all | bytes 196608 | tf_op jit(solution)/shard_map/all_to_all | solution.py:359
  28.9 0.0 copy-done
  28.9 1.6 %shard_map.93 = f32[8,16,384]{2,1,0:T(8,128)} custom-call(bf16[16,24,128]{2,1,0:T(8,128)(2,1)S(1)} %all_to_all.11.y, bf16[8,384,384]{2,1,0:T(8,128)(2,1)S(1)} %bitcast.7), custom_call_target="tpu_custom_call" | custom-call | flops 1000000000 | bytes 10000000 | tf_op jit(solution)/shard_map/pallas_call | solution.py:361
Async XLA Ops:
  1.2 27.7 %copy-start = (bf16[1,8,384,384]{3,2,1,0:T(8,128)(2,1)S(1)}, bf16[1,8,384,384]{3,2,1,0:T(8,128)(2,1)}, u32[]{:S(2)}) copy-start(bf16[1,8,384,384]{3,2,1,0:T(8,128)(2,1)} %param.16) | copy-start | bytes 7077892

commit v7 on v6

--- a/solution.py
+++ b/solution.py
@@ -1,5 +1,6 @@
 import functools
 import math
+import random
 
 import jax
 import jax.numpy as jnp
@@ -21,6 +22,18 @@
 
 BF = jnp.bfloat16
 F32 = jnp.float32
+
+
+FIRST, SECOND = 227, 147
+
+
+def arrangement(count, draw):
+    devices = list(range(count))
+    random.Random(draw).shuffle(devices)
+    places = [0] * count
+    for place, device in enumerate(devices):
+        places[device] = place
+    return places, devices
 
 
 def hold(x):
@@ -66,7 +79,13 @@
     return 2 * local * COMPS, local * COMPS
 
 
-def pack_body(vecs, local, slabs, spread, krylov, blade, iface, faces, *refs):
+def spot(places, slabs, device, side):
+    if slabs == 2:
+        return jnp.where(side == 0, places[2 * device], places[2 * device + 1])
+    return 2 * places[device] + side
+
+
+def pack_body(vecs, local, slabs, spread, places, krylov, blade, iface, faces, *refs):
     kept = (len(refs) - 8) // 2
     sources, out, pick, targets = refs[:kept], refs[kept], refs[kept + 1], refs[kept + 2 : 2 * kept + 2]
     rows, moved, classes, names, sides, sems = refs[-6:]
@@ -116,18 +135,18 @@
         moved[h * half : (h + 1) * half, :] = e
         rows[h * data : h * data + half, :] = e
         rows[h * data + half : (h + 1) * data, :] = v - shift_value * u
-    height = out.shape[2]
+    height = out.shape[1]
     mine = lax.axis_index("slab") if slabs == 2 else 0
     for v in range(vecs):
-        for at, source in ((mine, rows), (1 - mine, moved)):
+        for side, source in ((mine, rows), (1 - mine, moved)):
             chunk = source[pl.ds(v, height, stride=vecs), :].astype(BF)
             for i in range(spread):
-                out[v * spread + i, at] = chunk
+                out[spot(places, slabs, v * spread + i, side)] = chunk
     for move in rest:
         move.wait()
 
 
-def residual_body(slabs, wheel, local, width, x, *refs):
+def residual_body(slabs, wheel, local, width, places, leaving, x, *refs):
     ins, (out, rim, own, others, rows) = refs[:-5], refs[-5:]
     count = 1 if slabs == 2 else 2
     lows = ins[: 0 if slabs == 2 else count]
@@ -135,17 +154,17 @@
     nodes = neighbors.shape[1]
     halves = nodes // LANES
     sectors = wheel * local
-    height = x.shape[2]
+    height = x.shape[1]
     slab = lax.axis_index("slab")
     both, one = rows_of(local)
 
     mine = slab if slabs == 2 else 0
-    flat = (wheel * height, LANES)
-    own[...] = x[:, pl.ds(mine, 1)].astype(F32).reshape(flat)
-    extra = x[:, pl.ds(1 - mine, 1)].astype(F32).reshape(flat)
-    others[0] = extra
-    for i, ref in enumerate(lows):
-        others[1 + i] = ref[...].astype(F32).reshape(flat)
+    for w in range(wheel):
+        at = slice(w * height, (w + 1) * height)
+        own[at, :] = x[spot(places, slabs, w, mine)].astype(F32)
+        others[0, at, :] = x[spot(places, slabs, w, 1 - mine)].astype(F32)
+        for i, ref in enumerate(lows):
+            others[1 + i, at, :] = ref[places[w]].astype(F32)
     first = 0 if slabs == 2 else 1
 
     def field(source, rows_half, start):
@@ -239,15 +258,18 @@
         residual.append(part if gyro[c] is None else part - gyro[c])
     top, rest = split(jnp.concatenate(residual, axis=0))
     emit(1, top, top, rest)
-    out[...] = rows[...].astype(BF).reshape(out.shape)
-
-
-def apply_body(vecs, spread, y, precond, out, rows, stage, sems):
+    chunk = out.shape[1]
+    for p in range(pairs):
+        out[leaving[p]] = rows[p * chunk : (p + 1) * chunk, :].astype(BF)
+
+
+def apply_body(vecs, spread, places, y, precond, out, rows, stage, sems):
     kinds = 4 * COMPS
     per = LANES // GROUP
     chunk = y.shape[1]
     halves = chunk // kinds
-    rows[...] = y[...].astype(F32).reshape(rows.shape)
+    for w, place in enumerate(places):
+        rows[w * chunk : (w + 1) * chunk, :] = y[place].astype(F32)
     lane = lax.broadcasted_iota(jnp.int32, (vecs, LANES), 1)
     moves = []
     for h in range(halves):
@@ -300,13 +322,15 @@
     height = halves * both
     vmem = pl.BlockSpec(memory_space=pltpu.VMEM)
     anywhere = pl.BlockSpec(memory_space=pl.ANY)
+    places, devices = arrangement(wheel * slabs if slabs == 2 else wheel, FIRST)
+    leaving, receivers = arrangement(wheel, SECOND)
     params = pltpu.CompilerParams(vmem_limit_bytes=LIMIT)
 
     kept = (neighbors, stiffness, lumped_mass, jnp.asarray(transform(wheel, local)))
     packed, *tables = pl.pallas_call(
-        functools.partial(pack_body, vecs, local, slabs, spread),
+        functools.partial(pack_body, vecs, local, slabs, spread, places),
         out_shape=(
-            pltpu.VMEM((wheel, 2, height, LANES), BF),
+            pltpu.VMEM((wheel * 2, height, LANES), BF),
             pltpu.VMEM((nodes, 2 * width), BF),
             *(pltpu.VMEM(x.shape, x.dtype) for x in kept),
         ),
@@ -331,19 +355,20 @@
     )
     if slabs == 2:
         got = lax.all_to_all(
-            packed.reshape(wheel * slabs, height, LANES), ("wheel", "slab"), 0, 0, tiled=True
-        ).reshape(packed.shape)
+            packed, ("wheel", "slab"), 0, 0, axis_index_groups=[devices], tiled=True
+        )
         sides = ()
     else:
-        got = lax.all_to_all(packed, "wheel", 0, 0, tiled=True)
+        got = lax.all_to_all(packed, "wheel", 0, 0, axis_index_groups=[devices], tiled=True)
+        given = got[1::2]
         up = [(i, i + 1) for i in range(slabs - 1)]
         down = [(i + 1, i) for i in range(slabs - 1)]
-        sides = (lax.ppermute(got[:, 1], "slab", up), lax.ppermute(got[:, 1], "slab", down))
+        sides = (lax.ppermute(given, "slab", up), lax.ppermute(given, "slab", down))
 
     pairs = sectors // 2
     chunk = 4 * comps * halves
     sent = pl.pallas_call(
-        functools.partial(residual_body, slabs, wheel, local, width),
+        functools.partial(residual_body, slabs, wheel, local, width, places, leaving),
         out_shape=pltpu.VMEM((pairs, chunk, LANES), BF),
         in_specs=[vmem] * (1 + len(sides) + len(tables)),
         out_specs=vmem,
@@ -356,10 +381,10 @@
         compiler_params=params,
         cost_estimate=pl.CostEstimate(flops=1000000000, bytes_accessed=10000000, transcendentals=0),
     )(near(got), *(near(x) for x in sides), *(near(x) for x in tables))
-    back = lax.all_to_all(sent, "wheel", 0, 0, tiled=True)
+    back = lax.all_to_all(sent, "wheel", 0, 0, axis_index_groups=[receivers], tiled=True)
     owned, groups, order, _ = precond.shape
     out = pl.pallas_call(
-        functools.partial(apply_body, vecs, spread),
+        functools.partial(apply_body, vecs, spread, leaving),
         out_shape=jax.ShapeDtypeStruct((groups, vecs, order), F32),
         in_specs=[vmem, vmem],
         out_specs=anywhere,

time: 30.7 us -> 28 us (0.912)
  blocking collectives: 26.7 us -> 24.1 us
    all_to_all x2, blocking collectives: 26.7 us -> 24.1 us  [the longest x1 15.7 us: on_device(): lax.all_to_all(packed, ('wheel', 'slab'), 0, 0, axis_index_groups=[device...]
where the time goes in v7:
time: 28 us; the launch traced here: 27.8 us
  blocking collectives  24.1 us (86%)
  Pallas kernels  3.7 us (13%)
    all_to_all x1, blocking collectives, on_device(): lax.all_to_all(packed, ('wheel', 'slab'), 0, 0, axis_index_groups=[device...  15.7 us
    all_to_all x1, blocking collectives, on_device(): lax.all_to_all(sent, 'wheel', 0, 0, axis_index_groups=[receivers], tiled=...  8.36 us
    pallas_call x1, Pallas kernels, on_device(): pl.pallas_call(functools.partial(apply_body, vecs, spread, leaving), out_...  1.6 us
    pallas_call x1, Pallas kernels, on_device(): pl.pallas_call(functools.partial(pack_body, vecs, local, slabs, spread, p...  1.2 us
    pallas_call x1, Pallas kernels, on_device(): pl.pallas_call(functools.partial(residual_body, slabs, wheel, local, widt...  0.9 us

profile of v7, /device:TPU:0, one launch (start us, length us, event | category | flops | bytes accessed | tf_op | source)
XLA Modules:
  0.0 27.8 jit_solution(17580531064084394429)
XLA Ops:
  0.0 1.2 %shard_map.91 = (bf16[32,24,128]{2,1,0:T(8,128)(2,1)S(1)}, bf16[256,128]{1,0:T(8,128)(2,1)S(1)}, s32[8,256]{1,0:T(8,128)S(1)}, f32[3,3,8,256]{3,2,1,0:T(8,128)S(...) custom-call(f32[192,256]{1,0:T(8,128)} %bitcast.4, s32[2]{0:T(128)} %blade.1, s32[2,64]{1,0:T(2,128)} %iface.1, ...), custom_call_target="tpu_custom_call" | custom-call | flops 1000000000 | bytes 10000000 | tf_op jit(solution)/shard_map/pallas_call | solution.py:330
  1.2 0.0 copy-start
  1.2 15.7 %all_to_all.10.x = bf16[32,24,128]{2,1,0:T(8,128)(2,1)S(1)} all-to-all(bf16[32,24,128]{2,1,0:T(8,128)(2,1)S(1)} %get-tuple-element.11), channel_id=1, replica_groups={{4,10,15,12,20,9,6,18,17,31,0,27,16,19,28,30,24,5,8,3,1,22,13,23,7,14,2..., dimensions={0} | all-to-all | bytes 393216 | tf_op jit(solution)/shard_map/all_to_all | solution.py:357
  16.9 0.9 %shard_map.92 = bf16[16,24,128]{2,1,0:T(8,128)(2,1)S(1)} custom-call(bf16[32,24,128]{2,1,0:T(8,128)(2,1)S(1)} %all_to_all.10.x, bf16[256,128]{1,0:T(8,128)(2,1)S(1)} %get-tuple-element.12.refs_0_, s32[8,256]{1,0:T(8,128)S(1)} %get-tuple-element.13.refs_1_, f32[3,3,8,256]{3,2,1,0:T(8,128)S(1)} %get-tuple-element.14.refs_2_, ...), custom_call_target="tpu_custom_call" | custom-call | flops 1000000000 | bytes 10000000 | tf_op jit(solution)/shard_map/pallas_call | solution.py:370
  17.8 8.4 %all_to_all.11.y = bf16[16,24,128]{2,1,0:T(8,128)(2,1)S(1)} all-to-all(bf16[16,24,128]{2,1,0:T(8,128)(2,1)S(1)} %shard_map.92), channel_id=1, replica_groups={{22,16,2,10,0,6,20,26,30,4,24,18,14,12,28,8},{23,17,3,11,1,7,21,27,31,5..., dimensions={0} | all-to-all | bytes 196608 | tf_op jit(solution)/shard_map/all_to_all | solution.py:384
  26.2 0.0 copy-done
  26.2 1.6 %shard_map.93 = f32[8,16,384]{2,1,0:T(8,128)} custom-call(bf16[16,24,128]{2,1,0:T(8,128)(2,1)S(1)} %all_to_all.11.y, bf16[8,384,384]{2,1,0:T(8,128)(2,1)S(1)} %bitcast.3), custom_call_target="tpu_custom_call" | custom-call | flops 1000000000 | bytes 10000000 | tf_op jit(solution)/shard_map/pallas_call | solution.py:386
Async XLA Ops:
  1.2 25.0 %copy-start = (bf16[1,8,384,384]{3,2,1,0:T(8,128)(2,1)S(1)}, bf16[1,8,384,384]{3,2,1,0:T(8,128)(2,1)}, u32[]{:S(2)}) copy-start(bf16[1,8,384,384]{3,2,1,0:T(8,128)(2,1)} %param.16) | copy-start | bytes 7077892

commit v8 on v7

--- a/solution.py
+++ b/solution.py
@@ -1,6 +1,5 @@
 import functools
 import math
-import random
 
 import jax
 import jax.numpy as jnp
@@ -24,12 +23,16 @@
 F32 = jnp.float32
 
 
-FIRST, SECOND = 227, 147
+FIRST = 143277419789333953814782473828318468
+SECOND = 7671445128139
 
 
 def arrangement(count, draw):
-    devices = list(range(count))
-    random.Random(draw).shuffle(devices)
+    left = list(range(count))
+    devices = []
+    while left:
+        draw, pick = divmod(draw, len(left))
+        devices.append(left.pop(pick))
     places = [0] * count
     for place, device in enumerate(devices):
         places[device] = place

time: 28 us -> 27.7 us (0.989)
  blocking collectives: 24.1 us -> 23.8 us
where the time goes in v8:
time: 27.7 us; the launch traced here: 27.5 us
  blocking collectives  23.8 us (86%)
  Pallas kernels  3.7 us (13%)
    all_to_all x1, blocking collectives, on_device(): lax.all_to_all(packed, ('wheel', 'slab'), 0, 0, axis_index_groups=[device...  15.6 us
    all_to_all x1, blocking collectives, on_device(): lax.all_to_all(sent, 'wheel', 0, 0, axis_index_groups=[receivers], tiled=...  8.22 us
    pallas_call x1, Pallas kernels, on_device(): pl.pallas_call(functools.partial(apply_body, vecs, spread, leaving), out_...  1.6 us
    pallas_call x1, Pallas kernels, on_device(): pl.pallas_call(functools.partial(pack_body, vecs, local, slabs, spread, p...  1.2 us
    pallas_call x1, Pallas kernels, on_device(): pl.pallas_call(functools.partial(residual_body, slabs, wheel, local, widt...  0.9 us

profile of v8, /device:TPU:0, one launch (start us, length us, event | category | flops | bytes accessed | tf_op | source)
XLA Modules:
  0.0 27.5 jit_solution(11005301773263742154)
XLA Ops:
  0.0 1.2 %shard_map.91 = (bf16[32,24,128]{2,1,0:T(8,128)(2,1)S(1)}, bf16[256,128]{1,0:T(8,128)(2,1)S(1)}, s32[8,256]{1,0:T(8,128)S(1)}, f32[3,3,8,256]{3,2,1,0:T(8,128)S(...) custom-call(f32[192,256]{1,0:T(8,128)} %bitcast.4, s32[2]{0:T(128)} %blade.1, s32[2,64]{1,0:T(2,128)} %iface.1, ...), custom_call_target="tpu_custom_call" | custom-call | flops 1000000000 | bytes 10000000 | tf_op jit(solution)/shard_map/pallas_call | solution.py:333
  1.2 0.0 copy-start
  1.2 15.6 %all_to_all.10.x = bf16[32,24,128]{2,1,0:T(8,128)(2,1)S(1)} all-to-all(bf16[32,24,128]{2,1,0:T(8,128)(2,1)S(1)} %get-tuple-element.11), channel_id=1, replica_groups={{4,10,15,12,20,9,6,18,17,31,0,16,19,27,28,30,24,5,8,3,1,22,26,21,11,2,1..., dimensions={0} | all-to-all | bytes 393216 | tf_op jit(solution)/shard_map/all_to_all | solution.py:360
  16.8 0.9 %shard_map.92 = bf16[16,24,128]{2,1,0:T(8,128)(2,1)S(1)} custom-call(bf16[32,24,128]{2,1,0:T(8,128)(2,1)S(1)} %all_to_all.10.x, bf16[256,128]{1,0:T(8,128)(2,1)S(1)} %get-tuple-element.12.refs_0_, s32[8,256]{1,0:T(8,128)S(1)} %get-tuple-element.13.refs_1_, f32[3,3,8,256]{3,2,1,0:T(8,128)S(1)} %get-tuple-element.14.refs_2_, ...), custom_call_target="tpu_custom_call" | custom-call | flops 1000000000 | bytes 10000000 | tf_op jit(solution)/shard_map/pallas_call | solution.py:373
  17.7 8.2 %all_to_all.11.y = bf16[16,24,128]{2,1,0:T(8,128)(2,1)S(1)} all-to-all(bf16[16,24,128]{2,1,0:T(8,128)(2,1)S(1)} %shard_map.92), channel_id=1, replica_groups={{22,16,28,12,14,18,24,8,30,26,20,6,0,10,2,4},{23,17,29,13,15,19,25,9,31..., dimensions={0} | all-to-all | bytes 196608 | tf_op jit(solution)/shard_map/all_to_all | solution.py:387
  25.9 0.0 copy-done
  25.9 1.6 %shard_map.93 = f32[8,16,384]{2,1,0:T(8,128)} custom-call(bf16[16,24,128]{2,1,0:T(8,128)(2,1)S(1)} %all_to_all.11.y, bf16[8,384,384]{2,1,0:T(8,128)(2,1)S(1)} %bitcast.3), custom_call_target="tpu_custom_call" | custom-call | flops 1000000000 | bytes 10000000 | tf_op jit(solution)/shard_map/pallas_call | solution.py:389
Async XLA Ops:
  1.2 24.7 %copy-start = (bf16[1,8,384,384]{3,2,1,0:T(8,128)(2,1)S(1)}, bf16[1,8,384,384]{3,2,1,0:T(8,128)(2,1)}, u32[]{:S(2)}) copy-start(bf16[1,8,384,384]{3,2,1,0:T(8,128)(2,1)} %param.16) | copy-start | bytes 7077892

commit v9 on v8

--- a/solution.py
+++ b/solution.py
@@ -23,8 +23,8 @@
 F32 = jnp.float32
 
 
-FIRST = 143277419789333953814782473828318468
-SECOND = 7671445128139
+FIRST = 165202023144815051924973138721503180
+SECOND = 7663315406539
 
 
 def arrangement(count, draw):

time: 27.7 us -> 27.6 us (level)
  no operation moved by 1% of the time
where the time goes in v9:
time: 27.6 us; the launch traced here: 27.4 us
  blocking collectives  23.7 us (86%)
  Pallas kernels  3.7 us (13%)
    all_to_all x1, blocking collectives, on_device(): lax.all_to_all(packed, ('wheel', 'slab'), 0, 0, axis_index_groups=[device...  15.6 us
    all_to_all x1, blocking collectives, on_device(): lax.all_to_all(sent, 'wheel', 0, 0, axis_index_groups=[receivers], tiled=...  8.14 us
    pallas_call x1, Pallas kernels, on_device(): pl.pallas_call(functools.partial(apply_body, vecs, spread, leaving), out_...  1.6 us
    pallas_call x1, Pallas kernels, on_device(): pl.pallas_call(functools.partial(pack_body, vecs, local, slabs, spread, p...  1.2 us
    pallas_call x1, Pallas kernels, on_device(): pl.pallas_call(functools.partial(residual_body, slabs, wheel, local, widt...  0.9 us

profile of v9, /device:TPU:0, one launch (start us, length us, event | category | flops | bytes accessed | tf_op | source)
XLA Modules:
  0.0 27.4 jit_solution(8648481596154742399)
XLA Ops:
  0.0 1.2 %shard_map.91 = (bf16[32,24,128]{2,1,0:T(8,128)(2,1)S(1)}, bf16[256,128]{1,0:T(8,128)(2,1)S(1)}, s32[8,256]{1,0:T(8,128)S(1)}, f32[3,3,8,256]{3,2,1,0:T(8,128)S(...) custom-call(f32[192,256]{1,0:T(8,128)} %bitcast.4, s32[2]{0:T(128)} %blade.1, s32[2,64]{1,0:T(2,128)} %iface.1, ...), custom_call_target="tpu_custom_call" | custom-call | flops 1000000000 | bytes 10000000 | tf_op jit(solution)/shard_map/pallas_call | solution.py:333
  1.2 0.0 copy-start
  1.2 15.6 %all_to_all.10.x = bf16[32,24,128]{2,1,0:T(8,128)(2,1)S(1)} all-to-all(bf16[32,24,128]{2,1,0:T(8,128)(2,1)S(1)} %get-tuple-element.11), channel_id=1, replica_groups={{12,15,10,4,25,9,21,18,17,23,0,16,19,27,28,30,24,5,8,3,1,22,26,6,11,2,1..., dimensions={0} | all-to-all | bytes 393216 | tf_op jit(solution)/shard_map/all_to_all | solution.py:360
  16.8 0.9 %shard_map.92 = bf16[16,24,128]{2,1,0:T(8,128)(2,1)S(1)} custom-call(bf16[32,24,128]{2,1,0:T(8,128)(2,1)S(1)} %all_to_all.10.x, bf16[256,128]{1,0:T(8,128)(2,1)S(1)} %get-tuple-element.12.refs_0_, s32[8,256]{1,0:T(8,128)S(1)} %get-tuple-element.13.refs_1_, f32[3,3,8,256]{3,2,1,0:T(8,128)S(1)} %get-tuple-element.14.refs_2_, ...), custom_call_target="tpu_custom_call" | custom-call | flops 1000000000 | bytes 10000000 | tf_op jit(solution)/shard_map/pallas_call | solution.py:373
  17.7 8.1 %all_to_all.11.y = bf16[16,24,128]{2,1,0:T(8,128)(2,1)S(1)} all-to-all(bf16[16,24,128]{2,1,0:T(8,128)(2,1)S(1)} %shard_map.92), channel_id=1, replica_groups={{22,16,28,12,14,18,24,26,30,8,20,6,0,10,2,4},{23,17,29,13,15,19,25,27,3..., dimensions={0} | all-to-all | bytes 196608 | tf_op jit(solution)/shard_map/all_to_all | solution.py:387
  25.8 0.0 copy-done
  25.8 1.6 %shard_map.93 = f32[8,16,384]{2,1,0:T(8,128)} custom-call(bf16[16,24,128]{2,1,0:T(8,128)(2,1)S(1)} %all_to_all.11.y, bf16[8,384,384]{2,1,0:T(8,128)(2,1)S(1)} %bitcast.3), custom_call_target="tpu_custom_call" | custom-call | flops 1000000000 | bytes 10000000 | tf_op jit(solution)/shard_map/pallas_call | solution.py:389
Async XLA Ops:
  1.2 24.6 %copy-start = (bf16[1,8,384,384]{3,2,1,0:T(8,128)(2,1)S(1)}, bf16[1,8,384,384]{3,2,1,0:T(8,128)(2,1)}, u32[]{:S(2)}) copy-start(bf16[1,8,384,384]{3,2,1,0:T(8,128)(2,1)} %param.16) | copy-start | bytes 7077892

commit v10 on v9

--- a/solution.py
+++ b/solution.py
@@ -348,7 +348,7 @@
             pltpu.SemaphoreType.DMA((halves + 3 + len(kept),)),
         ],
         compiler_params=params,
-        cost_estimate=pl.CostEstimate(flops=1000000000, bytes_accessed=10000000, transcendentals=0),
+        cost_estimate=pl.CostEstimate(flops=10000000000, bytes_accessed=100000000, transcendentals=0),
     )(
         hold(krylov_block.reshape(states * local * comps * vecs, nodes)),
         hold(blade_class),
@@ -382,7 +382,7 @@
             pltpu.VMEM((pairs * chunk, LANES), F32),
         ],
         compiler_params=params,
-        cost_estimate=pl.CostEstimate(flops=1000000000, bytes_accessed=10000000, transcendentals=0),
+        cost_estimate=pl.CostEstimate(flops=10000000000, bytes_accessed=100000000, transcendentals=0),
     )(near(got), *(near(x) for x in sides), *(near(x) for x in tables))
     back = lax.all_to_all(sent, "wheel", 0, 0, axis_index_groups=[receivers], tiled=True)
     owned, groups, order, _ = precond.shape
@@ -397,7 +397,7 @@
             pltpu.SemaphoreType.DMA((groups,)),
         ],
         compiler_params=params,
-        cost_estimate=pl.CostEstimate(flops=1000000000, bytes_accessed=10000000, transcendentals=0),
+        cost_estimate=pl.CostEstimate(flops=10000000000, bytes_accessed=100000000, transcendentals=0),
     )(near(back), near(precond.reshape(groups, order, order)))
     return out.reshape(owned, groups, vecs, order)
 

time: 27.6 us -> 27.6 us (level)
  no operation moved by 1% of the time
where the time goes in v10:
time: 27.6 us; the launch traced here: 27.4 us
  blocking collectives  23.7 us (86%)
  Pallas kernels  3.7 us (13%)
    all_to_all x1, blocking collectives, on_device(): lax.all_to_all(packed, ('wheel', 'slab'), 0, 0, axis_index_groups=[device...  15.6 us
    all_to_all x1, blocking collectives, on_device(): lax.all_to_all(sent, 'wheel', 0, 0, axis_index_groups=[receivers], tiled=...  8.14 us
    pallas_call x1, Pallas kernels, on_device(): pl.pallas_call(functools.partial(apply_body, vecs, spread, leaving), out_...  1.6 us
    pallas_call x1, Pallas kernels, on_device(): pl.pallas_call(functools.partial(pack_body, vecs, local, slabs, spread, p...  1.2 us
    pallas_call x1, Pallas kernels, on_device(): pl.pallas_call(functools.partial(residual_body, slabs, wheel, local, widt...  0.9 us

profile of v10, /device:TPU:0, one launch (start us, length us, event | category | flops | bytes accessed | tf_op | source)
XLA Modules:
  0.0 27.4 jit_solution(12799597237451570034)
XLA Ops:
  0.0 1.2 %shard_map.91 = (bf16[32,24,128]{2,1,0:T(8,128)(2,1)S(1)}, bf16[256,128]{1,0:T(8,128)(2,1)S(1)}, s32[8,256]{1,0:T(8,128)S(1)}, f32[3,3,8,256]{3,2,1,0:T(8,128)S(...) custom-call(f32[192,256]{1,0:T(8,128)} %bitcast.4, s32[2]{0:T(128)} %blade.1, s32[2,64]{1,0:T(2,128)} %iface.1, ...), custom_call_target="tpu_custom_call" | custom-call | flops 10000000000 | bytes 100000000 | tf_op jit(solution)/shard_map/pallas_call | solution.py:333
  1.2 15.6 %all_to_all.10.x = bf16[32,24,128]{2,1,0:T(8,128)(2,1)S(1)} all-to-all(bf16[32,24,128]{2,1,0:T(8,128)(2,1)S(1)} %get-tuple-element.11), channel_id=1, replica_groups={{12,15,10,4,25,9,21,18,17,23,0,16,19,27,28,30,24,5,8,3,1,22,26,6,11,2,1..., dimensions={0} | all-to-all | bytes 393216 | tf_op jit(solution)/shard_map/all_to_all | solution.py:360
  16.8 0.0 copy-start
  16.8 0.9 %shard_map.92 = bf16[16,24,128]{2,1,0:T(8,128)(2,1)S(1)} custom-call(bf16[32,24,128]{2,1,0:T(8,128)(2,1)S(1)} %all_to_all.10.x, bf16[256,128]{1,0:T(8,128)(2,1)S(1)} %get-tuple-element.12.refs_0_, s32[8,256]{1,0:T(8,128)S(1)} %get-tuple-element.13.refs_1_, f32[3,3,8,256]{3,2,1,0:T(8,128)S(1)} %get-tuple-element.14.refs_2_, ...), custom_call_target="tpu_custom_call" | custom-call | flops 10000000000 | bytes 100000000 | tf_op jit(solution)/shard_map/pallas_call | solution.py:373
  17.7 8.1 %all_to_all.11.y = bf16[16,24,128]{2,1,0:T(8,128)(2,1)S(1)} all-to-all(bf16[16,24,128]{2,1,0:T(8,128)(2,1)S(1)} %shard_map.92), channel_id=1, replica_groups={{22,16,28,12,14,18,24,26,30,8,20,6,0,10,2,4},{23,17,29,13,15,19,25,27,3..., dimensions={0} | all-to-all | bytes 196608 | tf_op jit(solution)/shard_map/all_to_all | solution.py:387
  25.8 0.0 copy-done
  25.8 1.6 %shard_map.93 = f32[8,16,384]{2,1,0:T(8,128)} custom-call(bf16[16,24,128]{2,1,0:T(8,128)(2,1)S(1)} %all_to_all.11.y, bf16[8,384,384]{2,1,0:T(8,128)(2,1)S(1)} %bitcast.3), custom_call_target="tpu_custom_call" | custom-call | flops 10000000000 | bytes 100000000 | tf_op jit(solution)/shard_map/pallas_call | solution.py:389
Async XLA Ops:
  16.8 9.1 %copy-start = (bf16[1,8,384,384]{3,2,1,0:T(8,128)(2,1)S(1)}, bf16[1,8,384,384]{3,2,1,0:T(8,128)(2,1)}, u32[]{:S(2)}) copy-start(bf16[1,8,384,384]{3,2,1,0:T(8,128)(2,1)} %param.16) | copy-start | bytes 7077892
